TPU v7x, 256 devices: a whole 4x4x8 slice. The times are simulated.
256 devices in a mesh: level: 32 (over x, z), slab: 8 (over y, core).
Axes of the slice: x: 4, y: 4, z: 8, core: 2. Of those that a mesh axis runs over, the one named last changes fastest.
Arguments:
- trajectory: float32 [32, 8, 16, 32, 128], P('level', None, 'slab'), may hold values from -6 to 6
- first_latent: float32 [8, 16, 32, 128], P(None, 'slab'), may hold values from -6 to 6
- noise_draw: float32 [32, 8, 16, 32, 128], P('level', None, 'slab'), may hold values from -6 to 6
- w_in: bfloat16 [64, 8, 3, 3, 3], replicated, may hold values from -0.4375 to 0.4375
- bias_in: float32 [64], replicated, may hold values from -3 to 3
- level_bias: float32 [32, 64], P('level'), may hold values from -3 to 3
- w_out: bfloat16 [8, 64, 3, 3, 3], replicated, may hold values from -0.15625 to 0.15625
- bias_out: float32 [8], replicated, may hold values from -2 to 2
- drift_coef: float32 [32], P('level'), may hold values from -0.12 to -0.02
- eps_coef: float32 [32], P('level'), may hold values from 0.05 to 0.3
- noise_coef: float32 [32], P('level'), may hold values from 0.05 to 0.2
Outputs:
- next_states: float32 [32, 8, 16, 32, 128], P('level', None, 'slab')
All inputs are finite; a program needn't handle non-finite values.
Results may differ from a plain program's by a relative error of at most 0.0016.
Values may be sent and summed in bfloat16 or wider, within the bound.
No kernel may reach another device: no remote copies, remote signals or barrier semaphores. Data moves between devices by JAX's collectives and lax.ppermute only.
A program may use at most 64 MiB of HBM per device.

v0:
```python
import jax
import jax.numpy as jnp
from jax import lax
from jax.experimental import pallas as pl
from jax.experimental.pallas import tpu as pltpu
from jax.sharding import PartitionSpec as P

C, HID, H, W = 8, 64, 32, 128
BF, F32 = jnp.bfloat16, jnp.float32
ROWS = (H * C, 2 * W)


def swapped(ref, plane, block):
    tile = ref[:, plane, block * 8 : block * 8 + 8, :]
    return jnp.swapaxes(tile, 0, 1).reshape(64, W)


def tiles():
    for plane in range(2):
        for block in range(4):
            yield plane, block, slice(block * 64, block * 64 + 64), slice(plane * W, plane * W + W)


def latent_kernel(x_ref, out_ref):
    for plane, block, rows, lanes in tiles():
        out_ref[rows, lanes] = swapped(x_ref, plane, block).astype(BF)


def prepare_kernel(
    eps, scale, noise_ref, first_ref, w_in_ref, bias_in_ref, level_bias_ref, w_out_ref, bias_out_ref,
    fresh_ref, start_ref, kernel_in_ref, kernel_out_ref, first,
):
    same = lax.broadcasted_iota(jnp.int32, (C, C), 0) == lax.broadcasted_iota(jnp.int32, (C, C), 1)
    column = jnp.sum(jnp.where(same, jnp.broadcast_to(bias_out_ref[...], (C, C)), 0.0), axis=1, keepdims=True)
    shift = jnp.concatenate([jnp.broadcast_to(eps[0] * column, (C, W))] * 8, axis=0)
    for plane, block, rows, lanes in tiles():
        fresh_ref[rows, lanes] = scale[0] * swapped(noise_ref, plane, block) + shift
        first[rows, lanes] = swapped(first_ref, plane, block)
    own = pl.multiple_of(lax.axis_index("level") * C, C)
    start_ref[...] = first[pl.ds(own, C), :]

    bias = 0.5 * (bias_in_ref[...] + level_bias_ref[...])
    high = bias.astype(BF).astype(F32)
    middle = (bias - high).astype(BF).astype(F32)
    low = bias - high - middle
    nothing = jnp.zeros((C, HID), F32)
    row = lax.broadcasted_iota(jnp.int32, (C, HID), 0)
    biases = jnp.where(row == 0, high, jnp.where(row == 1, middle, jnp.where(row == 2, low, 0.0)))
    pieces = []
    for kh in range(3):
        pieces += [0.5 * w_in_ref[kd * 9 + kh * 3 + kw].astype(F32) for kd in range(3) for kw in range(3)]
        pieces.append(biases if kh == 1 else nothing)
    stacked = jnp.concatenate(pieces + [nothing] * 2, axis=0)
    stacked = jnp.concatenate([stacked, jnp.zeros_like(stacked)], axis=1)
    kernel_in_ref[...] = stacked.T[:HID, :240].astype(BF)
    rows_of = [
        jnp.concatenate([w_out_ref[kd * 9 + kh * 3 + kw].astype(F32) for kd in range(3) for kw in range(3)], axis=0)
        for kh in range(3)
    ]
    kernel_out_ref[...] = jnp.concatenate(rows_of, axis=1).astype(BF)


def edge_masks():
    lane = lax.broadcasted_iota(jnp.int32, (8, W), 1)
    return lane > 0, lane < W - 1


def from_left(tile, keep):
    return jnp.where(keep, pltpu.roll(tile, 1, 1), 0.0)


def from_right(tile, keep):
    return jnp.where(keep, pltpu.roll(tile, W - 1, 1), 0.0)


def taps_of(row, keeps):
    blocks = [row[:, p * W : p * W + W] for p in range(6)]
    shifted = (
        [from_left(b, keeps[0]) for b in blocks],
        blocks,
        [from_right(b, keeps[1]) for b in blocks],
    )
    pieces = [jnp.concatenate(shifted[kw][kd : kd + 4], axis=1) for kd in range(3) for kw in range(3)]
    pieces.append(jnp.ones((C, 4 * W), F32))
    return jnp.concatenate(pieces, axis=0).astype(BF)


def hidden_of(taps, kernel_in, inside):
    u = jnp.dot(kernel_in, taps, preferred_element_type=F32)
    u = jnp.concatenate([u[:, :W] * inside[0], u[:, W : 3 * W], u[:, 3 * W :] * inside[1]], axis=1)
    return (u + u * jnp.tanh(u)).astype(BF)


def predicted_of(hidden, kernel_out, keeps):
    y = jnp.dot(kernel_out, hidden, preferred_element_type=F32)
    planes = []
    for plane in range(2):
        sums = []
        for kw in range(3):
            parts = [
                y[(kd * 3 + kw) * C : (kd * 3 + kw) * C + C, (plane + kd) * W : (plane + kd) * W + W]
                for kd in range(3)
            ]
            sums.append(parts[0] + parts[1] + parts[2])
        planes.append(sums[1] + from_left(sums[0], keeps[0]) + from_right(sums[2], keeps[1]))
    return jnp.concatenate(planes, axis=1)


def step_kernel(
    slabs, drift, eps, below_ref, latent_ref, above_ref, kernel_in_ref, kernel_out_ref, fresh_ref,
    inc_ref, taps, hidden,
):
    keeps = edge_masks()
    slab = lax.axis_index("slab")
    inside = (jnp.where(slab > 0, 1.0, 0.0).astype(F32), jnp.where(slab < slabs - 1, 1.0, 0.0).astype(F32))
    kernel_in, kernel_out = kernel_in_ref[...], kernel_out_ref[...]
    ones = jnp.concatenate([jnp.zeros((72, 4 * W), F32), jnp.ones((8, 4 * W), F32)], axis=0).astype(BF)
    for edge in (0, H + 1):
        taps[edge] = ones
        hidden[edge] = jnp.zeros((HID, 4 * W), BF)

    def load(pair):
        rows = slice(pair * 16, pair * 16 + 16)
        for k in range(2):
            refs = (below_ref, latent_ref, above_ref)
            both = jnp.concatenate([ref[rows, :].astype(F32) for ref in refs], axis=1)
            taps[1 + pair * 2 + k] = taps_of(both[k * C : k * C + C], keeps)

    def widen(row):
        hidden[1 + row] = hidden_of(taps[row : row + 3].reshape(240, 4 * W), kernel_in, inside)

    def narrow(row):
        pred = predicted_of(hidden[row : row + 3].reshape(3 * HID, 4 * W), kernel_out, keeps)
        rows = slice(row * C, row * C + C)
        pair = latent_ref[row // 2 * 16 : row // 2 * 16 + 16, :].astype(F32)
        state = pair[row % 2 * C : row % 2 * C + C]
        inc_ref[rows, :] = (drift[0] * state + fresh_ref[rows, :] + eps[0] * pred).astype(inc_ref.dtype)

    for beat in range(H // 2 + 4):
        if beat < H // 2:
            load(beat)
        if 0 <= beat - 2 < H // 2:
            widen(2 * (beat - 2))
            widen(2 * (beat - 2) + 1)
        if 0 <= beat - 4:
            narrow(2 * (beat - 4))
            narrow(2 * (beat - 4) + 1)


def scan_kernel(inclusive, x_ref, start_ref, out_ref):
    total = start_ref[...]
    for pair in range(16):
        rows = slice(pair * 16, pair * 16 + 16)
        both = x_ref[rows, :].astype(F32)
        middle = total + both[:C]
        after = middle + both[C:]
        kept = [middle, after] if inclusive else [total, middle]
        out_ref[rows, :] = jnp.concatenate(kept, axis=0).astype(out_ref.dtype)
        total = after


def final_kernel(state_ref, out_ref):
    for plane, block, rows, lanes in tiles():
        out_ref[:, plane, block * 8 : block * 8 + 8, :] = jnp.swapaxes(state_ref[rows, lanes].reshape(8, C, W), 0, 1)


VMEM = pl.BlockSpec(memory_space=pltpu.VMEM)
SMEM = pl.BlockSpec(memory_space=pltpu.SMEM)


def near(array):
    return pltpu.with_memory_space_constraint(array, pltpu.VMEM)


def call(kernel, scalars, arrays, outs, scratch=(), name=None):
    return pl.pallas_call(
        kernel,
        out_shape=outs if len(outs) > 1 else outs[0],
        in_specs=[SMEM] * len(scalars) + [VMEM] * len(arrays),
        out_specs=[VMEM] * len(outs) if len(outs) > 1 else VMEM,
        scratch_shapes=scratch,
        name=name,
    )(*scalars, *arrays)


def on_device(trajectory, first_latent, noise_draw, w_in, bias_in, level_bias, w_out, bias_out, drift, eps, scale):
    slabs = lax.axis_size("slab")
    levels = lax.axis_size("level")
    up = [(i, i + 1) for i in range(slabs - 1)]
    down = [(i + 1, i) for i in range(slabs - 1)]

    latent = call(latent_kernel, (), (trajectory[0],), [pltpu.VMEM(ROWS, BF)], name="latent")
    fresh, start, kernel_in, kernel_out = call(
        prepare_kernel,
        (eps, scale),
        (
            noise_draw[0], first_latent,
            jnp.transpose(w_in, (2, 3, 4, 1, 0)).reshape(27, C, HID), bias_in[None], level_bias,
            jnp.transpose(w_out, (2, 3, 4, 0, 1)).reshape(27, C, HID), bias_out[None],
        ),
        [pltpu.VMEM(ROWS, F32), pltpu.VMEM((C, 2 * W), F32), pltpu.VMEM((HID, 240), BF), pltpu.VMEM((72, 3 * HID), BF)],
        [pltpu.VMEM(ROWS, F32)],
        name="prepare",
    )

    def step(latent, sent):
        below = lax.ppermute(latent, "slab", up)
        above = lax.ppermute(latent, "slab", down)
        inc = call(
            lambda *refs: step_kernel(slabs, *refs),
            (drift, eps),
            [near(a) for a in (below, latent, above, kernel_in, kernel_out, fresh)],
            [pltpu.VMEM(ROWS, sent)],
            [pltpu.VMEM((H + 2, 80, 4 * W), BF), pltpu.VMEM((H + 2, HID, 4 * W), BF)],
            name="step",
        )
        return exchange(inc)

    def exchange(array):
        return lax.all_to_all(array.reshape(levels, -1, 2 * W), "level", 0, 0).reshape(ROWS)

    def scan(inc, inclusive, kept):
        out = call(
            lambda *refs: scan_kernel(inclusive, *refs), (), [near(inc), near(start)], [pltpu.VMEM(ROWS, kept)], name="scan"
        )
        return exchange(out)

    latent = scan(step(latent, F32), False, BF)
    state = scan(step(latent, BF), True, F32)
    return call(final_kernel, (), (near(state),), [jax.ShapeDtypeStruct((C, 2, H, W), F32)], name="final")[None]


def solution(mesh):
    placed = (
        P("level", None, "slab", None, None),
        P(None, "slab", None, None),
        P("level", None, "slab", None, None),
        P(),
        P(),
        P("level", None),
        P(),
        P(),
        P("level"),
        P("level"),
        P("level"),
    )
    return jax.shard_map(
        on_device,
        mesh=mesh,
        in_specs=placed,
        out_specs=P("level", None, "slab", None, None),
        check_vma=False,
    )
```

profile of v0, /device:TPU:8, one launch (start us, length us, event | category | flops | bytes accessed | tf_op | source)
XLA Modules:
  0.0 90.9 jit_solution(3646784391871927122)
XLA Ops:
  0.0 1.0 %latent.1.refs_3_ = bf16[256,256]{1,0:T(8,128)(2,1)S(1)} custom-call(f32[8,2,32,128]{3,2,1,0:T(8,128)} %bitcast.29), custom_call_target="tpu_custom_call" | custom-call | tf_op jit(solution)/shard_map/latent/pallas_call | solution.py:176
  1.0 1.9 %collective-permute-start.1 = (bf16[256,256]{1,0:T(8,128)(2,1)S(1)}, bf16[256,256]{1,0:T(8,128)(2,1)S(1)}, u32[]{:S(2)}, u32[]{:S(2)}) collective-permute-start(bf16[256,256]{1,0:T(8,128)(2,1)S(1)} %latent.1.refs_3_), channel_id=1, source_target_pairs={{1,0},{2,1},{3,2},{4,3},{5,4},{6,5},{7,6},{9,8},{10,9},{11,10},{12... | collective-permute-start | bytes 393224 | tf_op jit(solution)/shard_map/ppermute | solution.py:208
  2.9 2.4 %collective-permute-start = (bf16[256,256]{1,0:T(8,128)(2,1)S(1)}, bf16[256,256]{1,0:T(8,128)(2,1)S(1)}, u32[]{:S(2)}, u32[]{:S(2)}) collective-permute-start(bf16[256,256]{1,0:T(8,128)(2,1)S(1)} %latent.1.refs_3_), channel_id=1, source_target_pairs={{0,1},{1,2},{2,3},{3,4},{4,5},{5,6},{6,7},{8,9},{9,10},{10,11},{11... | collective-permute-start | bytes 393224 | tf_op jit(solution)/shard_map/ppermute | solution.py:207
  7.3 1.2 %prepare.1 = (f32[256,256]{1,0:T(8,128)S(1)}, f32[8,256]{1,0:T(8,128)S(1)}, bf16[64,240]{1,0:T(8,128)(2,1)S(1)}, bf16[72,192]{1,0:T(8,128)(2,1)S(1)}) custom-call(f32[1]{0:T(128)S(6)} %copy.13.eps.refs_1_, f32[1]{0:T(128)S(6)} %copy.14.scale, f32[8,2,32,128]{3,2,1,0:T(8,128)} %bitcast.30, f32[8,2,32,128]{3,2,1,0:T(8,128)} %first_ref.1, ...), custom_call_target="tpu_custom_call" | custom-call | tf_op jit(solution)/shard_map/prepare/pallas_call | solution.py:176
  8.5 0.0 collective-permute-done.1.refs_4_
  8.6 1.2 %collective-permute-done.refs_2_ = bf16[256,256]{1,0:T(8,128)(2,1)S(1)} collective-permute-done((bf16[256,256]{1,0:T(8,128)(2,1)S(1)}, bf16[256,256]{1,0:T(8,128)(2,1)S(1)}, u32[]{:S(2)}, u32[]{:S(2)}) %collective-permute-start) | collective-permute-done | bytes 131104 | tf_op jit(solution)/shard_map/ppermute | solution.py:207
  9.8 2.7 %step.2 = f32[256,256]{1,0:T(8,128)S(1)} custom-call(f32[1]{0:T(128)S(6)} %copy.12.refs_0_, f32[1]{0:T(128)S(6)} %copy.13.eps.refs_1_, bf16[256,256]{1,0:T(8,128)(2,1)S(1)} %collective-permute-done.refs_2_, bf16[256,256]{1,0:T(8,128)(2,1)S(1)} %latent.1.refs_3_, bf16[256,256]{1,0:T(8,128)(2,1)S(1)} %collective-permute-done.1.refs_4_, ...), custom_call_target="tpu_custom_call" | custom-call | tf_op jit(solution)/shard_map/step/pallas_call | solution.py:176
  12.5 23.0 %all_to_all.20 = f32[32,8,256]{2,1,0:T(8,128)S(1)} all-to-all(f32[32,8,256]{2,1,0:T(8,128)S(1)} %bitcast.19), channel_id=1, replica_groups=mesh['level'=32,'slab'=8] {'level'}, dimensions={0} | all-to-all | bytes 524288 | tf_op jit(solution)/shard_map/all_to_all | solution.py:220
  35.5 15.2 %all_to_all.21 = bf16[32,8,256]{2,1,0:T(8,128)(2,1)S(1)} all-to-all(bf16[32,8,256]{2,1,0:T(8,128)(2,1)S(1)} %bitcast.24), channel_id=1, replica_groups=mesh['level'=32,'slab'=8] {'level'}, dimensions={0} | all-to-all | bytes 262144 | tf_op jit(solution)/shard_map/all_to_all | solution.py:220
  50.7 1.9 %collective-permute-start.3 = (bf16[256,256]{1,0:T(8,128)(2,1)S(1)}, bf16[256,256]{1,0:T(8,128)(2,1)S(1)}, u32[]{:S(2)}, u32[]{:S(2)}) collective-permute-start(bf16[256,256]{1,0:T(8,128)(2,1)S(1)} %bitcast.25), channel_id=1, source_target_pairs={{1,0},{2,1},{3,2},{4,3},{5,4},{6,5},{7,6},{9,8},{10,9},{11,10},{12... | collective-permute-start | bytes 393224 | tf_op jit(solution)/shard_map/ppermute | solution.py:208
  52.6 2.4 %collective-permute-start.2 = (bf16[256,256]{1,0:T(8,128)(2,1)S(1)}, bf16[256,256]{1,0:T(8,128)(2,1)S(1)}, u32[]{:S(2)}, u32[]{:S(2)}) collective-permute-start(bf16[256,256]{1,0:T(8,128)(2,1)S(1)} %bitcast.26), channel_id=1, source_target_pairs={{0,1},{1,2},{2,3},{3,4},{4,5},{5,6},{6,7},{8,9},{9,10},{10,11},{11... | collective-permute-start | bytes 393224 | tf_op jit(solution)/shard_map/ppermute | solution.py:207
  55.0 0.1 collective-permute-done.3.refs_4_
  55.1 3.8 %collective-permute-done.2.refs_2_ = bf16[256,256]{1,0:T(8,128)(2,1)S(1)} collective-permute-done((bf16[256,256]{1,0:T(8,128)(2,1)S(1)}, bf16[256,256]{1,0:T(8,128)(2,1)S(1)}, u32[]{:S(2)}, u32[]{:S(2)}) %collective-permute-start.2) | collective-permute-done | bytes 131104 | tf_op jit(solution)/shard_map/ppermute | solution.py:207
  58.9 2.7 %step.3 = bf16[256,256]{1,0:T(8,128)(2,1)S(1)} custom-call(f32[1]{0:T(128)S(6)} %copy.12.refs_0_, f32[1]{0:T(128)S(6)} %copy.13.eps.refs_1_, bf16[256,256]{1,0:T(8,128)(2,1)S(1)} %collective-permute-done.2.refs_2_, bf16[256,256]{1,0:T(8,128)(2,1)S(1)} %bitcast.27, bf16[256,256]{1,0:T(8,128)(2,1)S(1)} %collective-permute-done.3.refs_4_, ...), custom_call_target="tpu_custom_call" | custom-call | tf_op jit(solution)/shard_map/step/pallas_call | solution.py:176
  61.6 14.0 %all_to_all.22 = bf16[32,8,256]{2,1,0:T(8,128)(2,1)S(1)} all-to-all(bf16[32,8,256]{2,1,0:T(8,128)(2,1)S(1)} %bitcast.28), channel_id=1, replica_groups=mesh['level'=32,'slab'=8] {'level'}, dimensions={0} | all-to-all | bytes 262144 | tf_op jit(solution)/shard_map/all_to_all | solution.py:220
  75.7 14.5 %all_to_all.23 = f32[32,8,256]{2,1,0:T(8,128)S(1)} all-to-all(f32[32,8,256]{2,1,0:T(8,128)S(1)} %bitcast.21), channel_id=1, replica_groups=mesh['level'=32,'slab'=8] {'level'}, dimensions={0} | all-to-all | bytes 524288 | tf_op jit(solution)/shard_map/all_to_all | solution.py:220
  90.2 0.8 final.1
  (2 shorter events, 0.1 us)
Async XLA Ops:
  1.0 7.5 %collective-permute-start.1 = (bf16[256,256]{1,0:T(8,128)(2,1)S(1)}, bf16[256,256]{1,0:T(8,128)(2,1)S(1)}, u32[]{:S(2)}, u32[]{:S(2)}) collective-permute-start(bf16[256,256]{1,0:T(8,128)(2,1)S(1)} %latent.1.refs_3_), channel_id=1, source_target_pairs={{1,0},{2,1},{3,2},{4,3},{5,4},{6,5},{7,6},{9,8},{10,9},{11,10},{12... | collective-permute-start | bytes 393224 | tf_op jit(solution)/shard_map/ppermute | solution.py:208
  2.9 6.8 %collective-permute-start = (bf16[256,256]{1,0:T(8,128)(2,1)S(1)}, bf16[256,256]{1,0:T(8,128)(2,1)S(1)}, u32[]{:S(2)}, u32[]{:S(2)}) collective-permute-start(bf16[256,256]{1,0:T(8,128)(2,1)S(1)} %latent.1.refs_3_), channel_id=1, source_target_pairs={{0,1},{1,2},{2,3},{3,4},{4,5},{5,6},{6,7},{8,9},{9,10},{10,11},{11... | collective-permute-start | bytes 393224 | tf_op jit(solution)/shard_map/ppermute | solution.py:207
  50.7 4.4 %collective-permute-start.3 = (bf16[256,256]{1,0:T(8,128)(2,1)S(1)}, bf16[256,256]{1,0:T(8,128)(2,1)S(1)}, u32[]{:S(2)}, u32[]{:S(2)}) collective-permute-start(bf16[256,256]{1,0:T(8,128)(2,1)S(1)} %bitcast.25), channel_id=1, source_target_pairs={{1,0},{2,1},{3,2},{4,3},{5,4},{6,5},{7,6},{9,8},{10,9},{11,10},{12... | collective-permute-start | bytes 393224 | tf_op jit(solution)/shard_map/ppermute | solution.py:208
  52.6 6.3 %collective-permute-start.2 = (bf16[256,256]{1,0:T(8,128)(2,1)S(1)}, bf16[256,256]{1,0:T(8,128)(2,1)S(1)}, u32[]{:S(2)}, u32[]{:S(2)}) collective-permute-start(bf16[256,256]{1,0:T(8,128)(2,1)S(1)} %bitcast.26), channel_id=1, source_target_pairs={{0,1},{1,2},{2,3},{3,4},{4,5},{5,6},{6,7},{8,9},{9,10},{10,11},{11... | collective-permute-start | bytes 393224 | tf_op jit(solution)/shard_map/ppermute | solution.py:207
where the time goes:
time: 91.3 us; the launch traced here: 90.9 us
  blocking collectives  66.7 us (73%)
  starting transfers between devices  8.64 us (9%)
  Pallas kernels  8.52 us (9%)
  waiting for transfers between devices  5.07 us (6%)
  between operations  2 us (2%)
    all_to_all x4, blocking collectives, exchange(): lax.all_to_all(array.reshape(levels, -1, 2 * W), 'level', 0, 0)  66.7 us
    pallas_call x7, Pallas kernels, call(): pl.pallas_call(kernel, out_shape=outs if len(outs) > 1 else outs[0], in_s...  8.52 us
    ppermute x2, waiting for transfers between devices, step(): below = lax.ppermute(latent, 'slab', up)  4.99 us
    ppermute x2, starting transfers between devices, step(): below = lax.ppermute(latent, 'slab', up)  4.81 us
    ppermute x2, starting transfers between devices, step(): above = lax.ppermute(latent, 'slab', down)  3.83 us
  transfers between devices with their start and end apart: 4, of which 3 were waited for; matrix products, arithmetic and copies ran while one was open for 0% of the time, Pallas kernels for 1%

commit v1 on v0

--- a/solution.py
+++ b/solution.py
@@ -107,11 +107,12 @@
 
 
 def step_kernel(
-    slabs, drift, eps, below_ref, latent_ref, above_ref, kernel_in_ref, kernel_out_ref, fresh_ref,
+    slabs, drift, eps, paired_ref, latent_ref, crossed_ref, kernel_in_ref, kernel_out_ref, fresh_ref,
     inc_ref, taps, hidden,
 ):
     keeps = edge_masks()
     slab = lax.axis_index("slab")
+    odd = slab % 2 == 1
     inside = (jnp.where(slab > 0, 1.0, 0.0).astype(F32), jnp.where(slab < slabs - 1, 1.0, 0.0).astype(F32))
     kernel_in, kernel_out = kernel_in_ref[...], kernel_out_ref[...]
     ones = jnp.concatenate([jnp.zeros((72, 4 * W), F32), jnp.ones((8, 4 * W), F32)], axis=0).astype(BF)
@@ -121,9 +122,10 @@
 
     def load(pair):
         rows = slice(pair * 16, pair * 16 + 16)
+        paired, crossed = paired_ref[rows, :].astype(F32), crossed_ref[rows, :].astype(F32)
+        below, above = jnp.where(odd, paired, crossed), jnp.where(odd, crossed, paired)
+        both = jnp.concatenate([below, latent_ref[rows, :].astype(F32), above], axis=1)
         for k in range(2):
-            refs = (below_ref, latent_ref, above_ref)
-            both = jnp.concatenate([ref[rows, :].astype(F32) for ref in refs], axis=1)
             taps[1 + pair * 2 + k] = taps_of(both[k * C : k * C + C], keeps)
 
     def widen(row):
@@ -186,8 +188,8 @@
 def on_device(trajectory, first_latent, noise_draw, w_in, bias_in, level_bias, w_out, bias_out, drift, eps, scale):
     slabs = lax.axis_size("slab")
     levels = lax.axis_size("level")
-    up = [(i, i + 1) for i in range(slabs - 1)]
-    down = [(i + 1, i) for i in range(slabs - 1)]
+    pairs = [(i, i ^ 1) for i in range(slabs)]
+    crossings = [(i, j) for k in range(1, slabs - 1, 2) for i, j in ((k, k + 1), (k + 1, k))]
 
     latent = call(latent_kernel, (), (trajectory[0],), [pltpu.VMEM(ROWS, BF)], name="latent")
     fresh, start, kernel_in, kernel_out = call(
@@ -204,12 +206,12 @@
     )
 
     def step(latent, sent):
-        below = lax.ppermute(latent, "slab", up)
-        above = lax.ppermute(latent, "slab", down)
+        crossed = lax.ppermute(latent, "slab", crossings)
+        paired = lax.ppermute(latent, "slab", pairs)
         inc = call(
             lambda *refs: step_kernel(slabs, *refs),
             (drift, eps),
-            [near(a) for a in (below, latent, above, kernel_in, kernel_out, fresh)],
+            [near(a) for a in (paired, latent, crossed, kernel_in, kernel_out, fresh)],
             [pltpu.VMEM(ROWS, sent)],
             [pltpu.VMEM((H + 2, 80, 4 * W), BF), pltpu.VMEM((H + 2, HID, 4 * W), BF)],
             name="step",

time: 91.3 us -> 88.5 us (0.969)
  waiting for transfers between devices: 5.07 us -> 2.89 us
  starting transfers between devices: 8.64 us -> 7.07 us
    ppermute x4, waiting for transfers between devices: 5.07 us -> 2.89 us  [the longest x2 2.89 us: step(): crossed = lax.ppermute(latent, 'slab', crossings)]
    ppermute x4, starting transfers between devices: 8.64 us -> 7.07 us  [the longest x2 3.83 us: step(): crossed = lax.ppermute(latent, 'slab', crossings)]
  transfers between devices with their start and end apart: 4 -> 4, of which waited for: 3 -> 1; matrix products, arithmetic and copies ran while one was open for 0% -> 0% of each run, Pallas kernels for 1% -> 1%
where the time goes in v1:
time: 88.5 us; the launch traced here: 88.1 us
  blocking collectives  67.6 us (76%)
  Pallas kernels  8.55 us (10%)
  starting transfers between devices  7.07 us (8%)
  waiting for transfers between devices  2.89 us (3%)
  between operations  1.99 us (2%)
    all_to_all x4, blocking collectives, exchange(): lax.all_to_all(array.reshape(levels, -1, 2 * W), 'level', 0, 0)  67.6 us
    pallas_call x7, Pallas kernels, call(): pl.pallas_call(kernel, out_shape=outs if len(outs) > 1 else outs[0], in_s...  8.55 us
    ppermute x2, starting transfers between devices, step(): crossed = lax.ppermute(latent, 'slab', crossings)  3.83 us
    ppermute x2, starting transfers between devices, step(): paired = lax.ppermute(latent, 'slab', pairs)  3.24 us
    ppermute x2, waiting for transfers between devices, step(): crossed = lax.ppermute(latent, 'slab', crossings)  2.89 us
  transfers between devices with their start and end apart: 4, of which 1 were waited for; matrix products, arithmetic and copies ran while one was open for 0% of the time, Pallas kernels for 1%

profile of v1, /device:TPU:8, one launch (start us, length us, event | category | flops | bytes accessed | tf_op | source)
XLA Modules:
  0.0 88.1 jit_solution(2534578833189834868)
XLA Ops:
  0.0 1.0 %latent.1.refs_3_ = bf16[256,256]{1,0:T(8,128)(2,1)S(1)} custom-call(f32[8,2,32,128]{3,2,1,0:T(8,128)} %bitcast.29), custom_call_target="tpu_custom_call" | custom-call | tf_op jit(solution)/shard_map/latent/pallas_call | solution.py:178
  1.0 1.9 %collective-permute-start.1 = (bf16[256,256]{1,0:T(8,128)(2,1)S(1)}, bf16[256,256]{1,0:T(8,128)(2,1)S(1)}, u32[]{:S(2)}, u32[]{:S(2)}) collective-permute-start(bf16[256,256]{1,0:T(8,128)(2,1)S(1)} %latent.1.refs_3_), channel_id=1, source_target_pairs={{1,2},{2,1},{3,4},{4,3},{5,6},{6,5},{9,10},{10,9},{11,12},{12,11},... | collective-permute-start | bytes 393224 | tf_op jit(solution)/shard_map/ppermute | solution.py:209
  2.9 1.8 %collective-permute-start = (bf16[256,256]{1,0:T(8,128)(2,1)S(1)}, bf16[256,256]{1,0:T(8,128)(2,1)S(1)}, u32[]{:S(2)}, u32[]{:S(2)}) collective-permute-start(bf16[256,256]{1,0:T(8,128)(2,1)S(1)} %latent.1.refs_3_), channel_id=1, source_target_pairs={{0,1},{1,0},{2,3},{3,2},{4,5},{5,4},{6,7},{7,6},{8,9},{9,8},{10,11... | collective-permute-start | bytes 393224 | tf_op jit(solution)/shard_map/ppermute | solution.py:210
  6.7 1.2 %prepare.1 = (f32[256,256]{1,0:T(8,128)S(1)}, f32[8,256]{1,0:T(8,128)S(1)}, bf16[64,240]{1,0:T(8,128)(2,1)S(1)}, bf16[72,192]{1,0:T(8,128)(2,1)S(1)}) custom-call(f32[1]{0:T(128)S(6)} %copy.13.eps.refs_1_, f32[1]{0:T(128)S(6)} %copy.14.scale, f32[8,2,32,128]{3,2,1,0:T(8,128)} %bitcast.30, f32[8,2,32,128]{3,2,1,0:T(8,128)} %first_ref.1, ...), custom_call_target="tpu_custom_call" | custom-call | tf_op jit(solution)/shard_map/prepare/pallas_call | solution.py:178
  7.9 0.0 collective-permute-done.1.refs_4_
  7.9 0.0 collective-permute-done.refs_2_
  7.9 2.8 %step.2 = f32[256,256]{1,0:T(8,128)S(1)} custom-call(f32[1]{0:T(128)S(6)} %copy.12.refs_0_, f32[1]{0:T(128)S(6)} %copy.13.eps.refs_1_, bf16[256,256]{1,0:T(8,128)(2,1)S(1)} %collective-permute-done.refs_2_, bf16[256,256]{1,0:T(8,128)(2,1)S(1)} %latent.1.refs_3_, bf16[256,256]{1,0:T(8,128)(2,1)S(1)} %collective-permute-done.1.refs_4_, ...), custom_call_target="tpu_custom_call" | custom-call | tf_op jit(solution)/shard_map/step/pallas_call | solution.py:178
  10.7 23.6 %all_to_all.20 = f32[32,8,256]{2,1,0:T(8,128)S(1)} all-to-all(f32[32,8,256]{2,1,0:T(8,128)S(1)} %bitcast.19), channel_id=1, replica_groups=mesh['level'=32,'slab'=8] {'level'}, dimensions={0} | all-to-all | bytes 524288 | tf_op jit(solution)/shard_map/all_to_all | solution.py:222
  34.4 14.7 %all_to_all.21 = bf16[32,8,256]{2,1,0:T(8,128)(2,1)S(1)} all-to-all(bf16[32,8,256]{2,1,0:T(8,128)(2,1)S(1)} %bitcast.24), channel_id=1, replica_groups=mesh['level'=32,'slab'=8] {'level'}, dimensions={0} | all-to-all | bytes 262144 | tf_op jit(solution)/shard_map/all_to_all | solution.py:222
  49.0 1.9 %collective-permute-start.3 = (bf16[256,256]{1,0:T(8,128)(2,1)S(1)}, bf16[256,256]{1,0:T(8,128)(2,1)S(1)}, u32[]{:S(2)}, u32[]{:S(2)}) collective-permute-start(bf16[256,256]{1,0:T(8,128)(2,1)S(1)} %bitcast.25), channel_id=1, source_target_pairs={{1,2},{2,1},{3,4},{4,3},{5,6},{6,5},{9,10},{10,9},{11,12},{12,11},... | collective-permute-start | bytes 393224 | tf_op jit(solution)/shard_map/ppermute | solution.py:209
  51.0 1.5 %collective-permute-start.2 = (bf16[256,256]{1,0:T(8,128)(2,1)S(1)}, bf16[256,256]{1,0:T(8,128)(2,1)S(1)}, u32[]{:S(2)}, u32[]{:S(2)}) collective-permute-start(bf16[256,256]{1,0:T(8,128)(2,1)S(1)} %bitcast.26), channel_id=1, source_target_pairs={{0,1},{1,0},{2,3},{3,2},{4,5},{5,4},{6,7},{7,6},{8,9},{9,8},{10,11... | collective-permute-start | bytes 393224 | tf_op jit(solution)/shard_map/ppermute | solution.py:210
  52.4 2.9 %collective-permute-done.3.refs_4_ = bf16[256,256]{1,0:T(8,128)(2,1)S(1)} collective-permute-done((bf16[256,256]{1,0:T(8,128)(2,1)S(1)}, bf16[256,256]{1,0:T(8,128)(2,1)S(1)}, u32[]{:S(2)}, u32[]{:S(2)}) %collective-permute-start.3) | collective-permute-done | bytes 131104 | tf_op jit(solution)/shard_map/ppermute | solution.py:209
  55.3 0.0 collective-permute-done.2.refs_2_
  55.3 2.7 %step.3 = bf16[256,256]{1,0:T(8,128)(2,1)S(1)} custom-call(f32[1]{0:T(128)S(6)} %copy.12.refs_0_, f32[1]{0:T(128)S(6)} %copy.13.eps.refs_1_, bf16[256,256]{1,0:T(8,128)(2,1)S(1)} %collective-permute-done.2.refs_2_, bf16[256,256]{1,0:T(8,128)(2,1)S(1)} %bitcast.27, bf16[256,256]{1,0:T(8,128)(2,1)S(1)} %collective-permute-done.3.refs_4_, ...), custom_call_target="tpu_custom_call" | custom-call | tf_op jit(solution)/shard_map/step/pallas_call | solution.py:178
  58.0 13.8 %all_to_all.22 = bf16[32,8,256]{2,1,0:T(8,128)(2,1)S(1)} all-to-all(bf16[32,8,256]{2,1,0:T(8,128)(2,1)S(1)} %bitcast.28), channel_id=1, replica_groups=mesh['level'=32,'slab'=8] {'level'}, dimensions={0} | all-to-all | bytes 262144 | tf_op jit(solution)/shard_map/all_to_all | solution.py:222
  71.9 15.5 %all_to_all.23 = f32[32,8,256]{2,1,0:T(8,128)S(1)} all-to-all(f32[32,8,256]{2,1,0:T(8,128)S(1)} %bitcast.21), channel_id=1, replica_groups=mesh['level'=32,'slab'=8] {'level'}, dimensions={0} | all-to-all | bytes 524288 | tf_op jit(solution)/shard_map/all_to_all | solution.py:222
  87.3 0.8 final.1
  (2 shorter events, 0.1 us)
Async XLA Ops:
  1.0 6.9 %collective-permute-start.1 = (bf16[256,256]{1,0:T(8,128)(2,1)S(1)}, bf16[256,256]{1,0:T(8,128)(2,1)S(1)}, u32[]{:S(2)}, u32[]{:S(2)}) collective-permute-start(bf16[256,256]{1,0:T(8,128)(2,1)S(1)} %latent.1.refs_3_), channel_id=1, source_target_pairs={{1,2},{2,1},{3,4},{4,3},{5,6},{6,5},{9,10},{10,9},{11,12},{12,11},... | collective-permute-start | bytes 393224 | tf_op jit(solution)/shard_map/ppermute | solution.py:209
  2.9 5.0 %collective-permute-start = (bf16[256,256]{1,0:T(8,128)(2,1)S(1)}, bf16[256,256]{1,0:T(8,128)(2,1)S(1)}, u32[]{:S(2)}, u32[]{:S(2)}) collective-permute-start(bf16[256,256]{1,0:T(8,128)(2,1)S(1)} %latent.1.refs_3_), channel_id=1, source_target_pairs={{0,1},{1,0},{2,3},{3,2},{4,5},{5,4},{6,7},{7,6},{8,9},{9,8},{10,11... | collective-permute-start | bytes 393224 | tf_op jit(solution)/shard_map/ppermute | solution.py:210
  49.0 6.3 %collective-permute-start.3 = (bf16[256,256]{1,0:T(8,128)(2,1)S(1)}, bf16[256,256]{1,0:T(8,128)(2,1)S(1)}, u32[]{:S(2)}, u32[]{:S(2)}) collective-permute-start(bf16[256,256]{1,0:T(8,128)(2,1)S(1)} %bitcast.25), channel_id=1, source_target_pairs={{1,2},{2,1},{3,4},{4,3},{5,6},{6,5},{9,10},{10,9},{11,12},{12,11},... | collective-permute-start | bytes 393224 | tf_op jit(solution)/shard_map/ppermute | solution.py:209
  51.0 4.4 %collective-permute-start.2 = (bf16[256,256]{1,0:T(8,128)(2,1)S(1)}, bf16[256,256]{1,0:T(8,128)(2,1)S(1)}, u32[]{:S(2)}, u32[]{:S(2)}) collective-permute-start(bf16[256,256]{1,0:T(8,128)(2,1)S(1)} %bitcast.26), channel_id=1, source_target_pairs={{0,1},{1,0},{2,3},{3,2},{4,5},{5,4},{6,7},{7,6},{8,9},{9,8},{10,11... | collective-permute-start | bytes 393224 | tf_op jit(solution)/shard_map/ppermute | solution.py:210

commit v2 on v1

v2 whole, which is shorter than its diff:
```python
import jax
import jax.numpy as jnp
from jax import lax
from jax.experimental import pallas as pl
from jax.experimental.pallas import tpu as pltpu
from jax.sharding import PartitionSpec as P

C, HID, H, W = 8, 64, 32, 128
BF, F32 = jnp.bfloat16, jnp.float32
GROUP = 8
OWN = H // GROUP
EXT = OWN + 4
LANES = 2 * W
KEEP, EDGE = OWN * C, EXT * C
MESSAGE = EDGE + 2 * KEEP + 16
TAPS = 9 * C + C


def swapped(ref, plane, block):
    tile = ref[:, plane, block * 8 : block * 8 + 8, :]
    return jnp.swapaxes(tile, 0, 1).reshape(64, W)


def tiles():
    for plane in range(2):
        for block in range(4):
            yield plane, block, slice(block * 64, block * 64 + 64), slice(plane * W, plane * W + W)


def split(value, parts):
    pieces = []
    for _ in range(parts):
        pieces.append(value.astype(BF).astype(F32))
        value = value - pieces[-1]
    return pieces


def latent_kernel(x_ref, out_ref):
    for plane, block, rows, lanes in tiles():
        out_ref[rows, lanes] = swapped(x_ref, plane, block).astype(BF)


def stacked_kernel(pieces, pads):
    rows = []
    for kh in range(3):
        rows += pieces[kh] + [pads[kh]]
    return jnp.concatenate(rows, axis=0)


def turned(stacked):
    spare = jnp.zeros((256 - 3 * TAPS, W), F32)
    return jnp.concatenate([stacked, spare], axis=0).T[:HID, : 3 * TAPS].astype(BF)


def prepare_kernel(
    drift, eps, scale, noise_ref, first_ref, w_in_ref, bias_in_ref, level_bias_ref, w_out_ref, bias_out_ref,
    fresh_ref, start_ref, kernel_in_ref, spread_ref, kernel_out_ref, params_ref, first,
):
    same = lax.broadcasted_iota(jnp.int32, (C, C), 0) == lax.broadcasted_iota(jnp.int32, (C, C), 1)
    column = jnp.sum(jnp.where(same, jnp.broadcast_to(bias_out_ref[...], (C, C)), 0.0), axis=1, keepdims=True)
    shift = jnp.concatenate([jnp.broadcast_to(eps[0] * column, (C, W))] * 8, axis=0)
    edge = jnp.zeros((2 * C, LANES), F32)
    first[: 2 * C, :] = edge
    first[2 * C + H * C :, :] = edge
    for plane, block, rows, lanes in tiles():
        fresh_ref[rows, lanes] = scale[0] * swapped(noise_ref, plane, block) + shift
        first[rows.start + 2 * C : rows.stop + 2 * C, lanes] = swapped(first_ref, plane, block)
    own = pl.multiple_of(lax.axis_index("level") % GROUP * KEEP, KEEP)
    start_ref[...] = first[pl.ds(own, EDGE), :]

    bias = 0.5 * (bias_in_ref[...] + level_bias_ref[...])
    bias = jnp.concatenate([bias, jnp.zeros((1, LANES - HID), F32)], axis=1)
    rows = split(bias, 3)
    for scalar in (drift, eps):
        rows += split(jnp.full((1, LANES), scalar[0], F32), 3)
    index = lax.broadcasted_iota(jnp.int32, (16, LANES), 0)
    params = jnp.zeros((16, LANES), F32)
    for k, row in enumerate(rows):
        params = jnp.where(index == k, row, params)
    params_ref[...] = params.astype(BF)

    wide = jnp.zeros((C, W - HID), F32)
    pieces = [
        [
            jnp.concatenate([0.5 * w_in_ref[kd * 9 + kh * 3 + kw].astype(F32), wide], axis=1)
            for kd in range(3)
            for kw in range(3)
        ]
        for kh in range(3)
    ]
    nothing = jnp.zeros((C, W), F32)
    top = lax.broadcasted_iota(jnp.int32, (C, W), 0) == 0
    spread_ref[...] = stacked_kernel(pieces, [nothing] * 3)
    kernel_in_ref[...] = turned(stacked_kernel(pieces, [jnp.where(top, rows[kh][:, :W], 0.0) for kh in range(3)]))
    rows_of = [
        jnp.concatenate([w_out_ref[kd * 9 + kh * 3 + kw].astype(F32) for kd in range(3) for kw in range(3)], axis=0)
        for kh in range(3)
    ]
    kernel_out_ref[...] = jnp.concatenate(rows_of, axis=1).astype(BF)


def edge_masks():
    lane = lax.broadcasted_iota(jnp.int32, (C, W), 1)
    return lane > 0, lane < W - 1


def from_left(tile, keep):
    return jnp.where(keep, pltpu.roll(tile, 1, 1), 0.0)


def from_right(tile, keep):
    return jnp.where(keep, pltpu.roll(tile, W - 1, 1), 0.0)


def selector(slot):
    return jnp.where(lax.broadcasted_iota(jnp.int32, (C, 4 * W), 0) == slot, 1.0, 0.0).astype(F32)


def taps_of(row, keeps, chosen):
    blocks = [row[:, p * W : p * W + W] for p in range(6)]
    shifted = (
        [from_left(b, keeps[0]) for b in blocks],
        blocks,
        [from_right(b, keeps[1]) for b in blocks],
    )
    pieces = [jnp.concatenate(shifted[kw][kd : kd + 4], axis=1) for kd in range(3) for kw in range(3)]
    return jnp.concatenate(pieces + [chosen], axis=0).astype(BF)


def hidden_of(taps, kernel_in, inside, exists=None):
    u = jnp.dot(kernel_in, taps, preferred_element_type=F32)
    left, middle, right = u[:, :W] * inside[0], u[:, W : 3 * W], u[:, 3 * W :] * inside[1]
    u = jnp.concatenate([left, middle, right], axis=1)
    if exists is not None:
        u = u * exists
    return (u + u * jnp.tanh(u)).astype(BF)


def predicted_of(hidden, kernel_out, keeps):
    y = jnp.dot(kernel_out, hidden, preferred_element_type=F32)
    planes = []
    for plane in range(2):
        sums = []
        for kw in range(3):
            parts = [
                y[(kd * 3 + kw) * C : (kd * 3 + kw) * C + C, (plane + kd) * W : (plane + kd) * W + W]
                for kd in range(3)
            ]
            sums.append(parts[0] + parts[1] + parts[2])
        planes.append(sums[1] + from_left(sums[0], keeps[0]) + from_right(sums[2], keeps[1]))
    return jnp.concatenate(planes, axis=1)


def one_if(condition):
    return jnp.where(condition, 1.0, 0.0).astype(F32)


def slab_facts(slabs):
    slab = lax.axis_index("slab")
    return slab % 2 == 1, (one_if(slab > 0), one_if(slab < slabs - 1))


def six_planes(rows, odd, paired_ref, latent_ref, crossed_ref):
    paired, crossed = paired_ref[rows, :].astype(F32), crossed_ref[rows, :].astype(F32)
    below, above = jnp.where(odd, paired, crossed), jnp.where(odd, crossed, paired)
    return jnp.concatenate([below, latent_ref[rows, :].astype(F32), above], axis=1)


def first_step_kernel(
    slabs, drift, eps, paired_ref, latent_ref, crossed_ref, kernel_in_ref, kernel_out_ref, fresh_ref, params_ref,
    out_ref, taps, hidden,
):
    keeps = edge_masks()
    odd, inside = slab_facts(slabs)
    kernel_in, kernel_out = kernel_in_ref[...], kernel_out_ref[...]
    chosen = selector(0)
    empty = jnp.concatenate([jnp.zeros((9 * C, 4 * W), F32), chosen], axis=0).astype(BF)
    for edge in (0, H + 1):
        taps[edge] = empty
        hidden[edge] = jnp.zeros((HID, 4 * W), BF)
    out_ref[: 2 * C, :] = jnp.zeros((2 * C, LANES), BF)
    last = (GROUP - 1) * MESSAGE + EDGE
    out_ref[last - 2 * C : last, :] = jnp.zeros((2 * C, LANES), BF)
    for peer in range(GROUP):
        out_ref[(peer + 1) * MESSAGE - 16 : (peer + 1) * MESSAGE, :] = params_ref[...]

    def load(pair):
        both = six_planes(slice(pair * 16, pair * 16 + 16), odd, paired_ref, latent_ref, crossed_ref)
        for k in range(2):
            taps[1 + pair * 2 + k] = taps_of(both[k * C : k * C + C], keeps, chosen)

    def widen(row):
        hidden[1 + row] = hidden_of(taps[row : row + 3].reshape(3 * TAPS, 4 * W), kernel_in, inside)

    def narrow(pair):
        preds = [
            predicted_of(hidden[row : row + 3].reshape(3 * HID, 4 * W), kernel_out, keeps)
            for row in (2 * pair, 2 * pair + 1)
        ]
        rows = slice(pair * 16, pair * 16 + 16)
        fresh = fresh_ref[rows, :]
        inc = drift[0] * latent_ref[rows, :].astype(F32) + fresh + eps[0] * jnp.concatenate(preds, axis=0)
        high = inc.astype(BF)
        for peer in range(GROUP):
            at = 2 * pair - (OWN * peer - 2)
            if 0 <= at < EXT:
                base = peer * MESSAGE + at * C
                out_ref[base : base + 16, :] = high
        peer = 2 * pair // OWN
        base = peer * MESSAGE + EDGE + (2 * pair - OWN * peer) * C
        out_ref[base : base + 16, :] = (inc - high.astype(F32)).astype(BF)
        out_ref[base + KEEP : base + KEEP + 16, :] = fresh.astype(BF)

    for beat in range(H // 2 + 4):
        if beat < H // 2:
            load(beat)
        if 0 <= beat - 2 < H // 2:
            widen(2 * (beat - 2))
            widen(2 * (beat - 2) + 1)
        if 0 <= beat - 4:
            narrow(beat - 4)


def scan_kernel(x_ref, before_ref, total_ref):
    for block in range(EXT // 2):
        at = block * 16
        low = at - 2 * C
        total = jnp.zeros((16, LANES), F32)
        for k in range(GROUP):
            before_ref[k * EDGE + at : k * EDGE + at + 16, :] = total
            base = k * MESSAGE
            total = total + x_ref[base + at : base + at + 16, :].astype(F32)
            if 0 <= low < KEEP:
                total = total + x_ref[base + EDGE + low : base + EDGE + low + 16, :].astype(F32)
        high = total.astype(BF)
        total_ref[at : at + 16, :] = high
        if 0 <= low < KEEP:
            total_ref[EDGE + low : EDGE + low + 16, :] = (total - high.astype(F32)).astype(BF)


def tune_kernel(x_ref, spread_ref, kernel_in_ref, coefs_ref):
    params = [x_ref[(k + 1) * MESSAGE - 16 : (k + 1) * MESSAGE, :].astype(F32) for k in range(GROUP)]
    index = lax.broadcasted_iota(jnp.int32, (GROUP, LANES), 0)

    def gathered(row):
        out = jnp.zeros((GROUP, LANES), F32)
        for k in range(GROUP):
            out = jnp.where(index == k, params[k][row : row + 1], out)
        return out

    pieces = [
        [spread_ref[kh * TAPS + k * C : kh * TAPS + k * C + C, :] for k in range(9)] for kh in range(3)
    ]
    kernel_in_ref[...] = turned(stacked_kernel(pieces, [gathered(kh)[:, :W] for kh in range(3)]))
    coefs_ref[:GROUP, :] = gathered(3) + gathered(4) + gathered(5)
    coefs_ref[GROUP:, :] = gathered(6) + gathered(7) + gathered(8)


def state_kernel(start_ref, one_ref, two_ref, three_ref, before_ref, latent_ref):
    for block in range(EXT // 2):
        rows = slice(block * 16, block * 16 + 16)
        offset = start_ref[rows, :]
        for ref in (one_ref, two_ref, three_ref):
            offset = offset + ref[rows, :].astype(F32)
            if 2 * C <= rows.start < 2 * C + KEEP:
                offset = offset + ref[rows.start + EDGE - 2 * C : rows.stop + EDGE - 2 * C, :].astype(F32)
        for k in range(GROUP):
            at = slice(k * EDGE + rows.start, k * EDGE + rows.stop)
            latent_ref[at, :] = (offset + before_ref[at, :]).astype(BF)


def second_step_kernel(
    slabs, paired_ref, latent_ref, crossed_ref, kernel_in_ref, kernel_out_ref, x_ref, coefs_ref,
    sum_ref, total_ref, taps, hidden,
):
    keeps = edge_masks()
    odd, inside = slab_facts(slabs)
    part = lax.axis_index("level") % GROUP
    exists = {0: one_if(part > 0), EXT - 3: one_if(part < GROUP - 1)}
    kernel_in, kernel_out = kernel_in_ref[...], kernel_out_ref[...]
    chosen = [selector(k) for k in range(GROUP)]
    running = [jnp.zeros((16, LANES), F32) for _ in range(OWN // 2)]

    def load(level, pair):
        at = level * EDGE + pair * 16
        both = six_planes(slice(at, at + 16), odd, paired_ref, latent_ref, crossed_ref)
        for k in range(2):
            taps[level * EXT + pair * 2 + k] = taps_of(both[k * C : k * C + C], keeps, chosen[level])

    def widen(level, row):
        at = level * EXT + row
        hidden[level * (EXT - 2) + row] = hidden_of(
            taps[at : at + 3].reshape(3 * TAPS, 4 * W), kernel_in, inside, exists.get(row)
        )

    def narrow(level, pair):
        at = level * (EXT - 2) + 2 * pair
        preds = [
            predicted_of(hidden[row : row + 3].reshape(3 * HID, 4 * W), kernel_out, keeps) for row in (at, at + 1)
        ]
        base = level * EDGE + 2 * C + pair * 16
        fresh = level * MESSAGE + EDGE + KEEP + pair * 16
        inc = coefs_ref[level : level + 1, :] * latent_ref[base : base + 16, :].astype(F32)
        inc = inc + x_ref[fresh : fresh + 16, :].astype(F32)
        inc = inc + coefs_ref[GROUP + level : GROUP + level + 1, :] * jnp.concatenate(preds, axis=0)
        running[pair] = running[pair] + inc
        sum_ref[level * KEEP + pair * 16 : level * KEEP + pair * 16 + 16, :] = running[pair]
        if level == GROUP - 1:
            total_ref[pair * 16 : pair * 16 + 16, :] = running[pair]

    for beat in range(GROUP + 2):
        loads = [(load, beat, k) for k in range(EXT // 2)] if beat < GROUP else []
        widens = [(widen, beat - 1, k) for k in range(EXT - 2)] if 0 <= beat - 1 < GROUP else []
        narrows = [(narrow, beat - 2, k) for k in range(OWN // 2)] if 0 <= beat - 2 else []
        jobs = [((k + 0.5) / len(each), job) for each in (loads, widens, narrows) for k, job in enumerate(each)]
        for _, (work, *where) in sorted(jobs, key=lambda job: job[0]):
            work(*where)


def add_kernel(start_ref, one_ref, two_ref, three_ref, sum_ref, out_ref):
    offset = start_ref[2 * C : 2 * C + KEEP, :] + (one_ref[...] + two_ref[...] + three_ref[...])
    for k in range(GROUP):
        rows = slice(k * KEEP, k * KEEP + KEEP)
        out_ref[rows, :] = offset + sum_ref[rows, :]


def final_kernel(state_ref, out_ref):
    for plane, block, rows, lanes in tiles():
        out_ref[:, plane, block * 8 : block * 8 + 8, :] = jnp.swapaxes(state_ref[rows, lanes].reshape(8, C, W), 0, 1)


VMEM = pl.BlockSpec(memory_space=pltpu.VMEM)
SMEM = pl.BlockSpec(memory_space=pltpu.SMEM)


def near(*arrays):
    return [pltpu.with_memory_space_constraint(array, pltpu.VMEM) for array in arrays]


def call(kernel, scalars, arrays, outs, scratch=(), name=None):
    return pl.pallas_call(
        kernel,
        out_shape=outs if len(outs) > 1 else outs[0],
        in_specs=[SMEM] * len(scalars) + [VMEM] * len(arrays),
        out_specs=[VMEM] * len(outs) if len(outs) > 1 else VMEM,
        scratch_shapes=scratch,
        name=name,
    )(*scalars, *arrays)


def on_device(trajectory, first_latent, noise_draw, w_in, bias_in, level_bias, w_out, bias_out, drift, eps, scale):
    slabs = lax.axis_size("slab")
    levels = lax.axis_size("level")
    pairs = [(i, i ^ 1) for i in range(slabs)]
    crossings = [(i, j) for k in range(1, slabs - 1, 2) for i, j in ((k, k + 1), (k + 1, k))]
    groups = [list(range(k, k + GROUP)) for k in range(0, levels, GROUP)]

    def neighbours(latent):
        crossed = lax.ppermute(latent, "slab", crossings)
        return lax.ppermute(latent, "slab", pairs), latent, crossed

    def exchange(array):
        parts = array.reshape(GROUP, -1, LANES)
        return lax.all_to_all(parts, "level", 0, 0, axis_index_groups=groups).reshape(array.shape)

    def earlier_groups(total):
        return [
            lax.ppermute(total, "level", [(i, i + k) for i in range(levels - k)]) for k in range(GROUP, levels, GROUP)
        ]

    latent = call(latent_kernel, (), (trajectory[0],), [pltpu.VMEM((H * C, LANES), BF)], name="latent")
    fresh, start, kernel_in, spread, kernel_out, params = call(
        prepare_kernel,
        (drift, eps, scale),
        (
            noise_draw[0], first_latent,
            jnp.transpose(w_in, (2, 3, 4, 1, 0)).reshape(27, C, HID), bias_in[None], level_bias,
            jnp.transpose(w_out, (2, 3, 4, 0, 1)).reshape(27, C, HID), bias_out[None],
        ),
        [
            pltpu.VMEM((H * C, LANES), F32), pltpu.VMEM((EDGE, LANES), F32), pltpu.VMEM((HID, 3 * TAPS), BF),
            pltpu.VMEM((3 * TAPS, W), F32), pltpu.VMEM((9 * C, 3 * HID), BF), pltpu.VMEM((16, LANES), BF),
        ],
        [pltpu.VMEM(((H + 4) * C, LANES), F32)],
        name="prepare",
    )
    sent = call(
        lambda *refs: first_step_kernel(slabs, *refs),
        (drift, eps),
        near(*neighbours(latent), kernel_in, kernel_out, fresh, params),
        [pltpu.VMEM((GROUP * MESSAGE, LANES), BF)],
        [pltpu.VMEM((H + 2, TAPS, 4 * W), BF), pltpu.VMEM((H + 2, HID, 4 * W), BF)],
        name="first",
    )
    got = exchange(sent)
    before, total = call(
        scan_kernel, (), near(got),
        [pltpu.VMEM((GROUP * EDGE, LANES), F32), pltpu.VMEM((EDGE + KEEP, LANES), BF)], name="scan",
    )
    kernel_in, coefs = call(
        tune_kernel, (), near(got, spread),
        [pltpu.VMEM((HID, 3 * TAPS), BF), pltpu.VMEM((2 * GROUP, LANES), F32)], name="tune",
    )
    latent = call(
        state_kernel, (), near(start, *earlier_groups(total), before),
        [pltpu.VMEM((GROUP * EDGE, LANES), BF)], name="state",
    )
    sums, total = call(
        lambda *refs: second_step_kernel(slabs, *refs),
        (),
        near(*neighbours(latent), kernel_in, kernel_out, got, coefs),
        [pltpu.VMEM((GROUP * KEEP, LANES), F32), pltpu.VMEM((KEEP, LANES), F32)],
        [
            pltpu.VMEM((GROUP * EXT, TAPS, 4 * W), BF),
            pltpu.VMEM((GROUP * (EXT - 2), HID, 4 * W), BF),
        ],
        name="second",
    )
    state = call(
        add_kernel, (), near(start, *earlier_groups(total), sums), [pltpu.VMEM((GROUP * KEEP, LANES), F32)], name="add"
    )
    return call(
        final_kernel, (), near(exchange(state)), [jax.ShapeDtypeStruct((C, 2, H, W), F32)], name="final"
    )[None]


def solution(mesh):
    placed = (
        P("level", None, "slab", None, None),
        P(None, "slab", None, None),
        P("level", None, "slab", None, None),
        P(),
        P(),
        P("level", None),
        P(),
        P(),
        P("level"),
        P("level"),
        P("level"),
    )
    return jax.shard_map(
        on_device,
        mesh=mesh,
        in_specs=placed,
        out_specs=P("level", None, "slab", None, None),
        check_vma=False,
    )
```

time: 88.5 us -> 83.8 us (0.947)
  blocking collectives: 67.6 us -> 40.9 us
  starting transfers between devices: 7.07 us -> 22.8 us
  waiting for transfers between devices: 2.89 us -> 7.47 us
  Pallas kernels: 8.55 us -> 9.57 us
    all_to_all x4 -> x2, blocking collectives: 67.6 us -> 40.9 us  [exchange(): lax.all_to_all(parts, 'level', 0, 0, axis_index_groups=groups)]
    ppermute x4 -> x10, starting transfers between devices: 7.07 us -> 22.8 us  [the longest x6 15.7 us: earlier_groups(): lax.ppermute(total, 'level', [(i, i + k) for i in range(levels - k)])]
    ppermute x4 -> x10, waiting for transfers between devices: 2.89 us -> 7.47 us  [the longest x2 4.19 us: neighbours(): crossed = lax.ppermute(latent, 'slab', crossings)]
    pallas_call x7 -> x9, Pallas kernels: 8.55 us -> 9.57 us  [call(): pl.pallas_call(kernel, out_shape=outs if len(outs) > 1 else outs[0], in_s...]
  transfers between devices with their start and end apart: 4 -> 10, of which waited for: 1 -> 3; matrix products, arithmetic and copies ran while one was open for 0% -> 0% of each run, Pallas kernels for 1% -> 2%
where the time goes in v2:
time: 83.8 us; the launch traced here: 82.8 us
  blocking collectives  40.9 us (49%)
  starting transfers between devices  22.8 us (27%)
  Pallas kernels  9.57 us (11%)
  waiting for transfers between devices  7.47 us (9%)
  between operations  2.09 us (2%)
    all_to_all x2, blocking collectives, exchange(): lax.all_to_all(parts, 'level', 0, 0, axis_index_groups=groups)  40.9 us
    ppermute x6, starting transfers between devices, earlier_groups(): lax.ppermute(total, 'level', [(i, i + k) for i in range(levels - k)])  15.7 us
    pallas_call x9, Pallas kernels, call(): pl.pallas_call(kernel, out_shape=outs if len(outs) > 1 else outs[0], in_s...  9.57 us
    ppermute x2, waiting for transfers between devices, neighbours(): crossed = lax.ppermute(latent, 'slab', crossings)  4.19 us
    ppermute x2, starting transfers between devices, neighbours(): crossed = lax.ppermute(latent, 'slab', crossings)  3.84 us
    ppermute x6, waiting for transfers between devices, earlier_groups(): lax.ppermute(total, 'level', [(i, i + k) for i in range(levels - k)])  3.28 us
    ppermute x2, starting transfers between devices, neighbours(): return (lax.ppermute(latent, 'slab', pairs), latent, crossed)  3.24 us
  transfers between devices with their start and end apart: 10, of which 3 were waited for; matrix products, arithmetic and copies ran while one was open for 0% of the time, Pallas kernels for 2%

profile of v2, /device:TPU:8, one launch (start us, length us, event | category | flops | bytes accessed | tf_op | source)
XLA Modules:
  0.0 82.8 jit_solution(3824234986931101682)
XLA Ops:
  0.0 1.0 %latent.1.refs_3_ = bf16[256,256]{1,0:T(8,128)(2,1)S(1)} custom-call(f32[8,2,32,128]{3,2,1,0:T(8,128)} %bitcast.22), custom_call_target="tpu_custom_call" | custom-call | tf_op jit(solution)/shard_map/latent/pallas_call | solution.py:341
  1.0 1.9 %collective-permute-start.1 = (bf16[256,256]{1,0:T(8,128)(2,1)S(1)}, bf16[256,256]{1,0:T(8,128)(2,1)S(1)}, u32[]{:S(2)}, u32[]{:S(2)}) collective-permute-start(bf16[256,256]{1,0:T(8,128)(2,1)S(1)} %latent.1.refs_3_), channel_id=1, source_target_pairs={{1,2},{2,1},{3,4},{4,3},{5,6},{6,5},{9,10},{10,9},{11,12},{12,11},... | collective-permute-start | bytes 393224 | tf_op jit(solution)/shard_map/ppermute | solution.py:359
  2.9 1.8 %collective-permute-start = (bf16[256,256]{1,0:T(8,128)(2,1)S(1)}, bf16[256,256]{1,0:T(8,128)(2,1)S(1)}, u32[]{:S(2)}, u32[]{:S(2)}) collective-permute-start(bf16[256,256]{1,0:T(8,128)(2,1)S(1)} %latent.1.refs_3_), channel_id=1, source_target_pairs={{0,1},{1,0},{2,3},{3,2},{4,5},{5,4},{6,7},{7,6},{8,9},{9,8},{10,11... | collective-permute-start | bytes 393224 | tf_op jit(solution)/shard_map/ppermute | solution.py:360
  6.7 1.2 %prepare.1 = (f32[256,256]{1,0:T(8,128)S(1)}, f32[64,256]{1,0:T(8,128)S(1)}, bf16[64,240]{1,0:T(8,128)(2,1)S(1)}, f32[240,128]{1,0:T(8,128)S(1)}, bf16[72,192]{1...) custom-call(f32[1]{0:T(128)S(6)} %copy.12.drift.refs_0_, f32[1]{0:T(128)S(6)} %copy.13.eps.refs_1_, f32[1]{0:T(128)S(6)} %copy.14.scale, ...), custom_call_target="tpu_custom_call" | custom-call | tf_op jit(solution)/shard_map/prepare/pallas_call | solution.py:341
  7.9 0.0 collective-permute-done.1.refs_4_
  7.9 0.0 collective-permute-done.refs_2_
  7.9 2.7 %first.1 = bf16[1152,256]{1,0:T(8,128)(2,1)S(1)} custom-call(f32[1]{0:T(128)S(6)} %copy.12.drift.refs_0_, f32[1]{0:T(128)S(6)} %copy.13.eps.refs_1_, bf16[256,256]{1,0:T(8,128)(2,1)S(1)} %collective-permute-done.refs_2_, bf16[256,256]{1,0:T(8,128)(2,1)S(1)} %latent.1.refs_3_, bf16[256,256]{1,0:T(8,128)(2,1)S(1)} %collective-permute-done.1.refs_4_, ...), custom_call_target="tpu_custom_call" | custom-call | tf_op jit(solution)/shard_map/first/pallas_call | solution.py:341
  10.7 27.3 %all_to_all.10 = bf16[8,144,256]{2,1,0:T(8,128)(2,1)S(1)} all-to-all(bf16[8,144,256]{2,1,0:T(8,128)(2,1)S(1)} %bitcast.18), channel_id=1, replica_groups={{0,8,16,24,32,40,48,56},{64,72,80,88,96,104,112,120},{128,136,144,152,1..., dimensions={0} | all-to-all | bytes 1179648 | tf_op jit(solution)/shard_map/all_to_all | solution.py:364
  38.0 0.1 scan.1
  38.1 4.7 %collective-permute-start.4 = (bf16[96,256]{1,0:T(8,128)(2,1)S(1)}, bf16[96,256]{1,0:T(8,128)(2,1)S(1)}, u32[]{:S(2)}, u32[]{:S(2)}) collective-permute-start(bf16[96,256]{1,0:T(8,128)(2,1)S(1)} %get-tuple-element.22), channel_id=1, source_target_pairs={{0,192},{8,200},{16,208},{24,216},{32,224},{40,232},{48,240},{56,2... | collective-permute-start | bytes 147464 | tf_op jit(solution)/shard_map/ppermute | solution.py:368
  42.7 1.3 %collective-permute-start.3 = (bf16[96,256]{1,0:T(8,128)(2,1)S(1)}, bf16[96,256]{1,0:T(8,128)(2,1)S(1)}, u32[]{:S(2)}, u32[]{:S(2)}) collective-permute-start(bf16[96,256]{1,0:T(8,128)(2,1)S(1)} %get-tuple-element.22), channel_id=1, source_target_pairs={{0,128},{8,136},{16,144},{24,152},{32,160},{40,168},{48,176},{56,1... | collective-permute-start | bytes 147464 | tf_op jit(solution)/shard_map/ppermute | solution.py:368
  44.0 2.8 %collective-permute-start.2 = (bf16[96,256]{1,0:T(8,128)(2,1)S(1)}, bf16[96,256]{1,0:T(8,128)(2,1)S(1)}, u32[]{:S(2)}, u32[]{:S(2)}) collective-permute-start(bf16[96,256]{1,0:T(8,128)(2,1)S(1)} %get-tuple-element.22), channel_id=1, source_target_pairs={{0,64},{8,72},{16,80},{24,88},{32,96},{40,104},{48,112},{56,120},{... | collective-permute-start | bytes 147464 | tf_op jit(solution)/shard_map/ppermute | solution.py:368
  46.8 0.0 collective-permute-done.4.three_ref
  46.8 0.0 collective-permute-done.3.two_ref
  46.8 1.7 %collective-permute-done.2.one_ref = bf16[96,256]{1,0:T(8,128)(2,1)S(1)} collective-permute-done((bf16[96,256]{1,0:T(8,128)(2,1)S(1)}, bf16[96,256]{1,0:T(8,128)(2,1)S(1)}, u32[]{:S(2)}, u32[]{:S(2)}) %collective-permute-start.2) | collective-permute-done | bytes 49184 | tf_op jit(solution)/shard_map/ppermute | solution.py:368
  48.5 0.1 state.1.refs_1_
  48.6 1.9 %collective-permute-start.6 = (bf16[512,256]{1,0:T(8,128)(2,1)S(1)}, bf16[512,256]{1,0:T(8,128)(2,1)S(1)}, u32[]{:S(2)}, u32[]{:S(2)}) collective-permute-start(bf16[512,256]{1,0:T(8,128)(2,1)S(1)} %state.1.refs_1_), channel_id=1, source_target_pairs={{1,2},{2,1},{3,4},{4,3},{5,6},{6,5},{9,10},{10,9},{11,12},{12,11},... | collective-permute-start | bytes 786440 | tf_op jit(solution)/shard_map/ppermute | solution.py:359
  50.5 1.5 %collective-permute-start.5 = (bf16[512,256]{1,0:T(8,128)(2,1)S(1)}, bf16[512,256]{1,0:T(8,128)(2,1)S(1)}, u32[]{:S(2)}, u32[]{:S(2)}) collective-permute-start(bf16[512,256]{1,0:T(8,128)(2,1)S(1)} %state.1.refs_1_), channel_id=1, source_target_pairs={{0,1},{1,0},{2,3},{3,2},{4,5},{5,4},{6,7},{7,6},{8,9},{9,8},{10,11... | collective-permute-start | bytes 786440 | tf_op jit(solution)/shard_map/ppermute | solution.py:360
  52.0 0.1 tune.1
  52.1 4.2 %collective-permute-done.6.refs_2_ = bf16[512,256]{1,0:T(8,128)(2,1)S(1)} collective-permute-done((bf16[512,256]{1,0:T(8,128)(2,1)S(1)}, bf16[512,256]{1,0:T(8,128)(2,1)S(1)}, u32[]{:S(2)}, u32[]{:S(2)}) %collective-permute-start.6) | collective-permute-done | bytes 262176 | tf_op jit(solution)/shard_map/ppermute | solution.py:359
  56.3 0.0 collective-permute-done.5.refs_0_
  56.3 3.6 %second.1 = (f32[256,256]{1,0:T(8,128)S(1)}, f32[32,256]{1,0:T(8,128)S(1)}) custom-call(bf16[512,256]{1,0:T(8,128)(2,1)S(1)} %collective-permute-done.5.refs_0_, bf16[512,256]{1,0:T(8,128)(2,1)S(1)} %state.1.refs_1_, bf16[512,256]{1,0:T(8,128)(2,1)S(1)} %collective-permute-done.6.refs_2_, bf16[64,240]{1,0:T(8,128)(2,1)S(1)} %get-tuple-element.25.refs_3_, ...), custom_call_target="tpu_custom_call" | custom-call | tf_op jit(solution)/shard_map/second/pallas_call | solution.py:341
  59.9 3.0 %collective-permute-start.9 = (f32[32,256]{1,0:T(8,128)S(1)}, f32[32,256]{1,0:T(8,128)S(1)}, u32[]{:S(2)}, u32[]{:S(2)}) collective-permute-start(f32[32,256]{1,0:T(8,128)S(1)} %get-tuple-element.27), channel_id=1, source_target_pairs={{0,192},{8,200},{16,208},{24,216},{32,224},{40,232},{48,240},{56,2... | collective-permute-start | bytes 98312 | tf_op jit(solution)/shard_map/ppermute | solution.py:368
  62.9 2.0 %collective-permute-start.8 = (f32[32,256]{1,0:T(8,128)S(1)}, f32[32,256]{1,0:T(8,128)S(1)}, u32[]{:S(2)}, u32[]{:S(2)}) collective-permute-start(f32[32,256]{1,0:T(8,128)S(1)} %get-tuple-element.27), channel_id=1, source_target_pairs={{0,128},{8,136},{16,144},{24,152},{32,160},{40,168},{48,176},{56,1... | collective-permute-start | bytes 98312 | tf_op jit(solution)/shard_map/ppermute | solution.py:368
  64.8 2.1 %collective-permute-start.7 = (f32[32,256]{1,0:T(8,128)S(1)}, f32[32,256]{1,0:T(8,128)S(1)}, u32[]{:S(2)}, u32[]{:S(2)}) collective-permute-start(f32[32,256]{1,0:T(8,128)S(1)} %get-tuple-element.27), channel_id=1, source_target_pairs={{0,64},{8,72},{16,80},{24,88},{32,96},{40,104},{48,112},{56,120},{... | collective-permute-start | bytes 98312 | tf_op jit(solution)/shard_map/ppermute | solution.py:368
  66.9 0.0 collective-permute-done.9.three_ref
  66.9 0.0 collective-permute-done.8.two_ref
  66.9 1.6 %collective-permute-done.7.one_ref = f32[32,256]{1,0:T(8,128)S(1)} collective-permute-done((f32[32,256]{1,0:T(8,128)S(1)}, f32[32,256]{1,0:T(8,128)S(1)}, u32[]{:S(2)}, u32[]{:S(2)}) %collective-permute-start.7) | collective-permute-done | bytes 32800 | tf_op jit(solution)/shard_map/ppermute | solution.py:368
  68.5 13.6 %all_to_all.11 = f32[8,32,256]{2,1,0:T(8,128)S(1)} all-to-all(f32[8,32,256]{2,1,0:T(8,128)S(1)} %bitcast.19), channel_id=1, replica_groups={{0,8,16,24,32,40,48,56},{64,72,80,88,96,104,112,120},{128,136,144,152,1..., dimensions={0} | all-to-all | bytes 524288 | tf_op jit(solution)/shard_map/all_to_all | solution.py:364
  82.1 0.8 final.1
  (1 shorter events, 0.0 us)
Async XLA Ops:
  1.0 6.9 %collective-permute-start.1 = (bf16[256,256]{1,0:T(8,128)(2,1)S(1)}, bf16[256,256]{1,0:T(8,128)(2,1)S(1)}, u32[]{:S(2)}, u32[]{:S(2)}) collective-permute-start(bf16[256,256]{1,0:T(8,128)(2,1)S(1)} %latent.1.refs_3_), channel_id=1, source_target_pairs={{1,2},{2,1},{3,4},{4,3},{5,6},{6,5},{9,10},{10,9},{11,12},{12,11},... | collective-permute-start | bytes 393224 | tf_op jit(solution)/shard_map/ppermute | solution.py:359
  2.9 5.0 %collective-permute-start = (bf16[256,256]{1,0:T(8,128)(2,1)S(1)}, bf16[256,256]{1,0:T(8,128)(2,1)S(1)}, u32[]{:S(2)}, u32[]{:S(2)}) collective-permute-start(bf16[256,256]{1,0:T(8,128)(2,1)S(1)} %latent.1.refs_3_), channel_id=1, source_target_pairs={{0,1},{1,0},{2,3},{3,2},{4,5},{5,4},{6,7},{7,6},{8,9},{9,8},{10,11... | collective-permute-start | bytes 393224 | tf_op jit(solution)/shard_map/ppermute | solution.py:360
  38.1 8.7 %collective-permute-start.4 = (bf16[96,256]{1,0:T(8,128)(2,1)S(1)}, bf16[96,256]{1,0:T(8,128)(2,1)S(1)}, u32[]{:S(2)}, u32[]{:S(2)}) collective-permute-start(bf16[96,256]{1,0:T(8,128)(2,1)S(1)} %get-tuple-element.22), channel_id=1, source_target_pairs={{0,192},{8,200},{16,208},{24,216},{32,224},{40,232},{48,240},{56,2... | collective-permute-start | bytes 147464 | tf_op jit(solution)/shard_map/ppermute | solution.py:368
  42.7 4.1 %collective-permute-start.3 = (bf16[96,256]{1,0:T(8,128)(2,1)S(1)}, bf16[96,256]{1,0:T(8,128)(2,1)S(1)}, u32[]{:S(2)}, u32[]{:S(2)}) collective-permute-start(bf16[96,256]{1,0:T(8,128)(2,1)S(1)} %get-tuple-element.22), channel_id=1, source_target_pairs={{0,128},{8,136},{16,144},{24,152},{32,160},{40,168},{48,176},{56,1... | collective-permute-start | bytes 147464 | tf_op jit(solution)/shard_map/ppermute | solution.py:368
  44.0 4.5 %collective-permute-start.2 = (bf16[96,256]{1,0:T(8,128)(2,1)S(1)}, bf16[96,256]{1,0:T(8,128)(2,1)S(1)}, u32[]{:S(2)}, u32[]{:S(2)}) collective-permute-start(bf16[96,256]{1,0:T(8,128)(2,1)S(1)} %get-tuple-element.22), channel_id=1, source_target_pairs={{0,64},{8,72},{16,80},{24,88},{32,96},{40,104},{48,112},{56,120},{... | collective-permute-start | bytes 147464 | tf_op jit(solution)/shard_map/ppermute | solution.py:368
  48.6 7.7 %collective-permute-start.6 = (bf16[512,256]{1,0:T(8,128)(2,1)S(1)}, bf16[512,256]{1,0:T(8,128)(2,1)S(1)}, u32[]{:S(2)}, u32[]{:S(2)}) collective-permute-start(bf16[512,256]{1,0:T(8,128)(2,1)S(1)} %state.1.refs_1_), channel_id=1, source_target_pairs={{1,2},{2,1},{3,4},{4,3},{5,6},{6,5},{9,10},{10,9},{11,12},{12,11},... | collective-permute-start | bytes 786440 | tf_op jit(solution)/shard_map/ppermute | solution.py:359
  50.5 5.8 %collective-permute-start.5 = (bf16[512,256]{1,0:T(8,128)(2,1)S(1)}, bf16[512,256]{1,0:T(8,128)(2,1)S(1)}, u32[]{:S(2)}, u32[]{:S(2)}) collective-permute-start(bf16[512,256]{1,0:T(8,128)(2,1)S(1)} %state.1.refs_1_), channel_id=1, source_target_pairs={{0,1},{1,0},{2,3},{3,2},{4,5},{5,4},{6,7},{7,6},{8,9},{9,8},{10,11... | collective-permute-start | bytes 786440 | tf_op jit(solution)/shard_map/ppermute | solution.py:360
  59.9 7.1 %collective-permute-start.9 = (f32[32,256]{1,0:T(8,128)S(1)}, f32[32,256]{1,0:T(8,128)S(1)}, u32[]{:S(2)}, u32[]{:S(2)}) collective-permute-start(f32[32,256]{1,0:T(8,128)S(1)} %get-tuple-element.27), channel_id=1, source_target_pairs={{0,192},{8,200},{16,208},{24,216},{32,224},{40,232},{48,240},{56,2... | collective-permute-start | bytes 98312 | tf_op jit(solution)/shard_map/ppermute | solution.py:368
  62.9 4.1 %collective-permute-start.8 = (f32[32,256]{1,0:T(8,128)S(1)}, f32[32,256]{1,0:T(8,128)S(1)}, u32[]{:S(2)}, u32[]{:S(2)}) collective-permute-start(f32[32,256]{1,0:T(8,128)S(1)} %get-tuple-element.27), channel_id=1, source_target_pairs={{0,128},{8,136},{16,144},{24,152},{32,160},{40,168},{48,176},{56,1... | collective-permute-start | bytes 98312 | tf_op jit(solution)/shard_map/ppermute | solution.py:368
  64.8 3.7 %collective-permute-start.7 = (f32[32,256]{1,0:T(8,128)S(1)}, f32[32,256]{1,0:T(8,128)S(1)}, u32[]{:S(2)}, u32[]{:S(2)}) collective-permute-start(f32[32,256]{1,0:T(8,128)S(1)} %get-tuple-element.27), channel_id=1, source_target_pairs={{0,64},{8,72},{16,80},{24,88},{32,96},{40,104},{48,112},{56,120},{... | collective-permute-start | bytes 98312 | tf_op jit(solution)/shard_map/ppermute | solution.py:368

commit v3 on v2

--- a/solution.py
+++ b/solution.py
@@ -12,7 +12,7 @@
 EXT = OWN + 4
 LANES = 2 * W
 KEEP, EDGE = OWN * C, EXT * C
-MESSAGE = EDGE + 2 * KEEP + 16
+MESSAGE = EDGE + KEEP + C
 TAPS = 9 * C + C
 
 
@@ -53,31 +53,34 @@
 
 
 def prepare_kernel(
-    drift, eps, scale, noise_ref, first_ref, w_in_ref, bias_in_ref, level_bias_ref, w_out_ref, bias_out_ref,
-    fresh_ref, start_ref, kernel_in_ref, spread_ref, kernel_out_ref, params_ref, first,
+    drift_ref, eps_ref, scale_ref, x_ref, noise_ref, first_ref, w_in_ref, bias_in_ref, level_bias_ref, w_out_ref, bias_out_ref,
+    base_ref, fresh_ref, start_ref, kernel_in_ref, spread_ref, kernel_out_ref, params_ref, first,
 ):
     same = lax.broadcasted_iota(jnp.int32, (C, C), 0) == lax.broadcasted_iota(jnp.int32, (C, C), 1)
+    drift, eps, scale = (jnp.full((1, W), ref[0], F32) for ref in (drift_ref, eps_ref, scale_ref))
     column = jnp.sum(jnp.where(same, jnp.broadcast_to(bias_out_ref[...], (C, C)), 0.0), axis=1, keepdims=True)
-    shift = jnp.concatenate([jnp.broadcast_to(eps[0] * column, (C, W))] * 8, axis=0)
+    shift = jnp.concatenate([eps * jnp.broadcast_to(column, (C, W))] * 8, axis=0)
     edge = jnp.zeros((2 * C, LANES), F32)
     first[: 2 * C, :] = edge
     first[2 * C + H * C :, :] = edge
     for plane, block, rows, lanes in tiles():
-        fresh_ref[rows, lanes] = scale[0] * swapped(noise_ref, plane, block) + shift
+        fresh = scale * swapped(noise_ref, plane, block) + shift
+        fresh_ref[rows, lanes] = fresh
+        base_ref[rows, lanes] = drift * swapped(x_ref, plane, block) + fresh
         first[rows.start + 2 * C : rows.stop + 2 * C, lanes] = swapped(first_ref, plane, block)
     own = pl.multiple_of(lax.axis_index("level") % GROUP * KEEP, KEEP)
     start_ref[...] = first[pl.ds(own, EDGE), :]
 
     bias = 0.5 * (bias_in_ref[...] + level_bias_ref[...])
-    bias = jnp.concatenate([bias, jnp.zeros((1, LANES - HID), F32)], axis=1)
+    bias = jnp.concatenate([bias, jnp.zeros((1, W - HID), F32)], axis=1)
     rows = split(bias, 3)
-    for scalar in (drift, eps):
-        rows += split(jnp.full((1, LANES), scalar[0], F32), 3)
-    index = lax.broadcasted_iota(jnp.int32, (16, LANES), 0)
-    params = jnp.zeros((16, LANES), F32)
-    for k, row in enumerate(rows):
-        params = jnp.where(index == k, row, params)
-    params_ref[...] = params.astype(BF)
+    index = lax.broadcasted_iota(jnp.int32, (C, W), 0)
+    left = right = jnp.zeros((C, W), F32)
+    for k, row in enumerate(rows + split(drift, 3)):
+        left = jnp.where(index == k, row, left)
+    for k, row in enumerate(split(eps, 3)):
+        right = jnp.where(index == 3 + k, row, right)
+    params_ref[...] = jnp.concatenate([left, right], axis=1).astype(BF)
 
     wide = jnp.zeros((C, W - HID), F32)
     pieces = [
@@ -91,7 +94,7 @@
     nothing = jnp.zeros((C, W), F32)
     top = lax.broadcasted_iota(jnp.int32, (C, W), 0) == 0
     spread_ref[...] = stacked_kernel(pieces, [nothing] * 3)
-    kernel_in_ref[...] = turned(stacked_kernel(pieces, [jnp.where(top, rows[kh][:, :W], 0.0) for kh in range(3)]))
+    kernel_in_ref[...] = turned(stacked_kernel(pieces, [jnp.where(top, rows[kh], 0.0) for kh in range(3)]))
     rows_of = [
         jnp.concatenate([w_out_ref[kd * 9 + kh * 3 + kw].astype(F32) for kd in range(3) for kw in range(3)], axis=0)
         for kh in range(3)
@@ -129,11 +132,10 @@
 
 def hidden_of(taps, kernel_in, inside, exists=None):
     u = jnp.dot(kernel_in, taps, preferred_element_type=F32)
-    left, middle, right = u[:, :W] * inside[0], u[:, W : 3 * W], u[:, 3 * W :] * inside[1]
-    u = jnp.concatenate([left, middle, right], axis=1)
+    out = (u + u * jnp.tanh(u)).astype(BF)
     if exists is not None:
-        u = u * exists
-    return (u + u * jnp.tanh(u)).astype(BF)
+        out = out * jnp.concatenate([exists] * 4, axis=1)
+    return jnp.concatenate([out[:, :W] * inside[0], out[:, W : 3 * W], out[:, 3 * W :] * inside[1]], axis=1)
 
 
 def predicted_of(hidden, kernel_out, keeps):
@@ -152,7 +154,7 @@
 
 
 def one_if(condition):
-    return jnp.where(condition, 1.0, 0.0).astype(F32)
+    return jnp.broadcast_to(jnp.where(condition, 1.0, 0.0).astype(F32), (1, W)).astype(BF)
 
 
 def slab_facts(slabs):
@@ -160,19 +162,20 @@
     return slab % 2 == 1, (one_if(slab > 0), one_if(slab < slabs - 1))
 
 
-def six_planes(rows, odd, paired_ref, latent_ref, crossed_ref):
-    paired, crossed = paired_ref[rows, :].astype(F32), crossed_ref[rows, :].astype(F32)
+def six_planes(odd, paired, own, crossed):
     below, above = jnp.where(odd, paired, crossed), jnp.where(odd, crossed, paired)
-    return jnp.concatenate([below, latent_ref[rows, :].astype(F32), above], axis=1)
+    return jnp.concatenate([below, own, above], axis=1)
 
 
 def first_step_kernel(
-    slabs, drift, eps, paired_ref, latent_ref, crossed_ref, kernel_in_ref, kernel_out_ref, fresh_ref, params_ref,
+    slabs, paired_ref, latent_ref, crossed_ref, kernel_in_ref, kernel_out_ref, base_ref, fresh_ref, params_ref,
     out_ref, taps, hidden,
 ):
     keeps = edge_masks()
     odd, inside = slab_facts(slabs)
     kernel_in, kernel_out = kernel_in_ref[...], kernel_out_ref[...]
+    eps = sum(params_ref[...].astype(F32)[row : row + 1, W:] for row in (3, 4, 5))
+    eps = jnp.concatenate([eps, eps], axis=1)
     chosen = selector(0)
     empty = jnp.concatenate([jnp.zeros((9 * C, 4 * W), F32), chosen], axis=0).astype(BF)
     for edge in (0, H + 1):
@@ -182,10 +185,11 @@
     last = (GROUP - 1) * MESSAGE + EDGE
     out_ref[last - 2 * C : last, :] = jnp.zeros((2 * C, LANES), BF)
     for peer in range(GROUP):
-        out_ref[(peer + 1) * MESSAGE - 16 : (peer + 1) * MESSAGE, :] = params_ref[...]
+        out_ref[(peer + 1) * MESSAGE - C : (peer + 1) * MESSAGE, :] = params_ref[...]
 
     def load(pair):
-        both = six_planes(slice(pair * 16, pair * 16 + 16), odd, paired_ref, latent_ref, crossed_ref)
+        rows = slice(pair * 16, pair * 16 + 16)
+        both = six_planes(odd, *[ref[rows, :].astype(F32) for ref in (paired_ref, latent_ref, crossed_ref)])
         for k in range(2):
             taps[1 + pair * 2 + k] = taps_of(both[k * C : k * C + C], keeps, chosen)
 
@@ -198,18 +202,16 @@
             for row in (2 * pair, 2 * pair + 1)
         ]
         rows = slice(pair * 16, pair * 16 + 16)
-        fresh = fresh_ref[rows, :]
-        inc = drift[0] * latent_ref[rows, :].astype(F32) + fresh + eps[0] * jnp.concatenate(preds, axis=0)
-        high = inc.astype(BF)
+        inc = base_ref[rows, :] + eps * jnp.concatenate(preds, axis=0)
+        known = (inc - fresh_ref[rows, :]).astype(BF)
         for peer in range(GROUP):
             at = 2 * pair - (OWN * peer - 2)
             if 0 <= at < EXT:
                 base = peer * MESSAGE + at * C
-                out_ref[base : base + 16, :] = high
+                out_ref[base : base + 16, :] = known if 2 <= at < 2 + OWN else inc.astype(BF)
         peer = 2 * pair // OWN
         base = peer * MESSAGE + EDGE + (2 * pair - OWN * peer) * C
-        out_ref[base : base + 16, :] = (inc - high.astype(F32)).astype(BF)
-        out_ref[base + KEEP : base + KEEP + 16, :] = fresh.astype(BF)
+        out_ref[base : base + 16, :] = (inc - known.astype(F32)).astype(BF)
 
     for beat in range(H // 2 + 4):
         if beat < H // 2:
@@ -227,7 +229,8 @@
         low = at - 2 * C
         total = jnp.zeros((16, LANES), F32)
         for k in range(GROUP):
-            before_ref[k * EDGE + at : k * EDGE + at + 16, :] = total
+            rows = slice(k * EDGE + at, k * EDGE + at + 16)
+            before_ref[rows, :] = total
             base = k * MESSAGE
             total = total + x_ref[base + at : base + at + 16, :].astype(F32)
             if 0 <= low < KEEP:
@@ -238,8 +241,25 @@
             total_ref[EDGE + low : EDGE + low + 16, :] = (total - high.astype(F32)).astype(BF)
 
 
+def state_kernel(start_ref, one_ref, two_ref, three_ref, before_ref, state_ref, latent_ref):
+    for block in range(EXT // 2):
+        rows = slice(block * 16, block * 16 + 16)
+        low = rows.start - 2 * C
+        offset = start_ref[rows, :]
+        for ref in (one_ref, two_ref, three_ref):
+            offset = offset + ref[rows, :].astype(F32)
+            if 0 <= low < KEEP:
+                offset = offset + ref[EDGE + low : EDGE + low + 16, :].astype(F32)
+        for k in range(GROUP):
+            at = slice(k * EDGE + rows.start, k * EDGE + rows.stop)
+            state = offset + before_ref[at, :]
+            latent_ref[at, :] = state.astype(BF)
+            if 0 <= low < KEEP:
+                state_ref[k * KEEP + low : k * KEEP + low + 16, :] = state
+
+
 def tune_kernel(x_ref, spread_ref, kernel_in_ref, coefs_ref):
-    params = [x_ref[(k + 1) * MESSAGE - 16 : (k + 1) * MESSAGE, :].astype(F32) for k in range(GROUP)]
+    params = [x_ref[(k + 1) * MESSAGE - C : (k + 1) * MESSAGE, :].astype(F32) for k in range(GROUP)]
     index = lax.broadcasted_iota(jnp.int32, (GROUP, LANES), 0)
 
     def gathered(row):
@@ -252,25 +272,13 @@
         [spread_ref[kh * TAPS + k * C : kh * TAPS + k * C + C, :] for k in range(9)] for kh in range(3)
     ]
     kernel_in_ref[...] = turned(stacked_kernel(pieces, [gathered(kh)[:, :W] for kh in range(3)]))
-    coefs_ref[:GROUP, :] = gathered(3) + gathered(4) + gathered(5)
-    coefs_ref[GROUP:, :] = gathered(6) + gathered(7) + gathered(8)
-
-
-def state_kernel(start_ref, one_ref, two_ref, three_ref, before_ref, latent_ref):
-    for block in range(EXT // 2):
-        rows = slice(block * 16, block * 16 + 16)
-        offset = start_ref[rows, :]
-        for ref in (one_ref, two_ref, three_ref):
-            offset = offset + ref[rows, :].astype(F32)
-            if 2 * C <= rows.start < 2 * C + KEEP:
-                offset = offset + ref[rows.start + EDGE - 2 * C : rows.stop + EDGE - 2 * C, :].astype(F32)
-        for k in range(GROUP):
-            at = slice(k * EDGE + rows.start, k * EDGE + rows.stop)
-            latent_ref[at, :] = (offset + before_ref[at, :]).astype(BF)
+    coefs = gathered(3) + gathered(4) + gathered(5)
+    coefs_ref[:GROUP, :] = jnp.concatenate([coefs[:, :W]] * 2, axis=1)
+    coefs_ref[GROUP:, :] = jnp.concatenate([coefs[:, W:]] * 2, axis=1)
 
 
 def second_step_kernel(
-    slabs, paired_ref, latent_ref, crossed_ref, kernel_in_ref, kernel_out_ref, x_ref, coefs_ref,
+    slabs, paired_ref, latent_ref, crossed_ref, kernel_in_ref, kernel_out_ref, x_ref, coefs_ref, state_ref,
     sum_ref, total_ref, taps, hidden,
 ):
     keeps = edge_masks()
@@ -283,7 +291,8 @@
 
     def load(level, pair):
         at = level * EDGE + pair * 16
-        both = six_planes(slice(at, at + 16), odd, paired_ref, latent_ref, crossed_ref)
+        refs = (paired_ref, latent_ref, crossed_ref)
+        both = six_planes(odd, *[ref[at : at + 16, :].astype(F32) for ref in refs])
         for k in range(2):
             taps[level * EXT + pair * 2 + k] = taps_of(both[k * C : k * C + C], keeps, chosen[level])
 
@@ -298,9 +307,9 @@
         preds = [
             predicted_of(hidden[row : row + 3].reshape(3 * HID, 4 * W), kernel_out, keeps) for row in (at, at + 1)
         ]
-        base = level * EDGE + 2 * C + pair * 16
-        fresh = level * MESSAGE + EDGE + KEEP + pair * 16
-        inc = coefs_ref[level : level + 1, :] * latent_ref[base : base + 16, :].astype(F32)
+        base = level * KEEP + pair * 16
+        fresh = level * MESSAGE + EDGE + pair * 16
+        inc = coefs_ref[level : level + 1, :] * state_ref[base : base + 16, :]
         inc = inc + x_ref[fresh : fresh + 16, :].astype(F32)
         inc = inc + coefs_ref[GROUP + level : GROUP + level + 1, :] * jnp.concatenate(preds, axis=0)
         running[pair] = running[pair] + inc
@@ -337,15 +346,15 @@
     return [pltpu.with_memory_space_constraint(array, pltpu.VMEM) for array in arrays]
 
 
-def call(kernel, scalars, arrays, outs, scratch=(), name=None):
+def call(kernel, arrays, outs, scratch=(), name=None, scalars=0):
     return pl.pallas_call(
         kernel,
         out_shape=outs if len(outs) > 1 else outs[0],
-        in_specs=[SMEM] * len(scalars) + [VMEM] * len(arrays),
+        in_specs=[SMEM] * scalars + [VMEM] * (len(arrays) - scalars),
         out_specs=[VMEM] * len(outs) if len(outs) > 1 else VMEM,
         scratch_shapes=scratch,
         name=name,
-    )(*scalars, *arrays)
+    )(*arrays)
 
 
 def on_device(trajectory, first_latent, noise_draw, w_in, bias_in, level_bias, w_out, bias_out, drift, eps, scale):
@@ -368,47 +377,47 @@
             lax.ppermute(total, "level", [(i, i + k) for i in range(levels - k)]) for k in range(GROUP, levels, GROUP)
         ]
 
-    latent = call(latent_kernel, (), (trajectory[0],), [pltpu.VMEM((H * C, LANES), BF)], name="latent")
-    fresh, start, kernel_in, spread, kernel_out, params = call(
+    latent = call(latent_kernel, (trajectory[0],), [pltpu.VMEM((H * C, LANES), BF)], name="latent")
+    base, fresh, start, kernel_in, spread, kernel_out, params = call(
         prepare_kernel,
-        (drift, eps, scale),
         (
-            noise_draw[0], first_latent,
+            drift, eps, scale,
+            trajectory[0], noise_draw[0], first_latent,
             jnp.transpose(w_in, (2, 3, 4, 1, 0)).reshape(27, C, HID), bias_in[None], level_bias,
             jnp.transpose(w_out, (2, 3, 4, 0, 1)).reshape(27, C, HID), bias_out[None],
         ),
         [
-            pltpu.VMEM((H * C, LANES), F32), pltpu.VMEM((EDGE, LANES), F32), pltpu.VMEM((HID, 3 * TAPS), BF),
-            pltpu.VMEM((3 * TAPS, W), F32), pltpu.VMEM((9 * C, 3 * HID), BF), pltpu.VMEM((16, LANES), BF),
+            pltpu.VMEM((H * C, LANES), F32), pltpu.VMEM((H * C, LANES), F32), pltpu.VMEM((EDGE, LANES), F32),
+            pltpu.VMEM((HID, 3 * TAPS), BF),
+            pltpu.VMEM((3 * TAPS, W), F32), pltpu.VMEM((9 * C, 3 * HID), BF), pltpu.VMEM((C, LANES), BF),
         ],
         [pltpu.VMEM(((H + 4) * C, LANES), F32)],
         name="prepare",
+        scalars=3,
     )
     sent = call(
         lambda *refs: first_step_kernel(slabs, *refs),
-        (drift, eps),
-        near(*neighbours(latent), kernel_in, kernel_out, fresh, params),
+        near(*neighbours(latent), kernel_in, kernel_out, base, fresh, params),
         [pltpu.VMEM((GROUP * MESSAGE, LANES), BF)],
         [pltpu.VMEM((H + 2, TAPS, 4 * W), BF), pltpu.VMEM((H + 2, HID, 4 * W), BF)],
         name="first",
     )
     got = exchange(sent)
     before, total = call(
-        scan_kernel, (), near(got),
+        scan_kernel, near(got),
         [pltpu.VMEM((GROUP * EDGE, LANES), F32), pltpu.VMEM((EDGE + KEEP, LANES), BF)], name="scan",
     )
     kernel_in, coefs = call(
-        tune_kernel, (), near(got, spread),
+        tune_kernel, near(got, spread),
         [pltpu.VMEM((HID, 3 * TAPS), BF), pltpu.VMEM((2 * GROUP, LANES), F32)], name="tune",
     )
-    latent = call(
-        state_kernel, (), near(start, *earlier_groups(total), before),
-        [pltpu.VMEM((GROUP * EDGE, LANES), BF)], name="state",
+    state, latent = call(
+        state_kernel, near(start, *earlier_groups(total), before),
+        [pltpu.VMEM((GROUP * KEEP, LANES), F32), pltpu.VMEM((GROUP * EDGE, LANES), BF)], name="state",
     )
     sums, total = call(
         lambda *refs: second_step_kernel(slabs, *refs),
-        (),
-        near(*neighbours(latent), kernel_in, kernel_out, got, coefs),
+        near(*neighbours(latent), kernel_in, kernel_out, got, coefs, state),
         [pltpu.VMEM((GROUP * KEEP, LANES), F32), pltpu.VMEM((KEEP, LANES), F32)],
         [
             pltpu.VMEM((GROUP * EXT, TAPS, 4 * W), BF),
@@ -417,10 +426,10 @@
         name="second",
     )
     state = call(
-        add_kernel, (), near(start, *earlier_groups(total), sums), [pltpu.VMEM((GROUP * KEEP, LANES), F32)], name="add"
+        add_kernel, near(start, *earlier_groups(total), sums), [pltpu.VMEM((GROUP * KEEP, LANES), F32)], name="add"
     )
     return call(
-        final_kernel, (), near(exchange(state)), [jax.ShapeDtypeStruct((C, 2, H, W), F32)], name="final"
+        final_kernel, near(exchange(state)), [jax.ShapeDtypeStruct((C, 2, H, W), F32)], name="final"
     )[None]
 
 

time: 83.8 us -> 80.3 us (0.958)
  blocking collectives: 40.9 us -> 37.4 us
    all_to_all x2, blocking collectives: 40.9 us -> 37.4 us  [exchange(): lax.all_to_all(parts, 'level', 0, 0, axis_index_groups=groups)]
where the time goes in v3:
time: 80.3 us; the launch traced here: 79.4 us
  blocking collectives  37.4 us (47%)
  starting transfers between devices  22.8 us (28%)
  Pallas kernels  9.6 us (12%)
  waiting for transfers between devices  7.49 us (9%)
  between operations  2.1 us (3%)
    all_to_all x2, blocking collectives, exchange(): lax.all_to_all(parts, 'level', 0, 0, axis_index_groups=groups)  37.4 us
    ppermute x6, starting transfers between devices, earlier_groups(): lax.ppermute(total, 'level', [(i, i + k) for i in range(levels - k)])  15.8 us
    pallas_call x9, Pallas kernels, call(): pl.pallas_call(kernel, out_shape=outs if len(outs) > 1 else outs[0], in_s...  9.6 us
    ppermute x2, waiting for transfers between devices, neighbours(): crossed = lax.ppermute(latent, 'slab', crossings)  4.2 us
    ppermute x2, starting transfers between devices, neighbours(): crossed = lax.ppermute(latent, 'slab', crossings)  3.84 us
    ppermute x6, waiting for transfers between devices, earlier_groups(): lax.ppermute(total, 'level', [(i, i + k) for i in range(levels - k)])  3.28 us
    ppermute x2, starting transfers between devices, neighbours(): return (lax.ppermute(latent, 'slab', pairs), latent, crossed)  3.24 us
  transfers between devices with their start and end apart: 10, of which 3 were waited for; matrix products, arithmetic and copies ran while one was open for 0% of the time, Pallas kernels for 2%

profile of v3, /device:TPU:8, one launch (start us, length us, event | category | flops | bytes accessed | tf_op | source)
XLA Modules:
  0.0 79.4 jit_solution(7039265554843678382)
XLA Ops:
  0.0 1.0 %latent.1.refs_1_ = bf16[256,256]{1,0:T(8,128)(2,1)S(1)} custom-call(f32[8,2,32,128]{3,2,1,0:T(8,128)} %bitcast.21), custom_call_target="tpu_custom_call" | custom-call | tf_op jit(solution)/shard_map/latent/pallas_call | solution.py:350
  1.0 1.9 %collective-permute-start.1 = (bf16[256,256]{1,0:T(8,128)(2,1)S(1)}, bf16[256,256]{1,0:T(8,128)(2,1)S(1)}, u32[]{:S(2)}, u32[]{:S(2)}) collective-permute-start(bf16[256,256]{1,0:T(8,128)(2,1)S(1)} %latent.1.refs_1_), channel_id=1, source_target_pairs={{1,2},{2,1},{3,4},{4,3},{5,6},{6,5},{9,10},{10,9},{11,12},{12,11},... | collective-permute-start | bytes 393224 | tf_op jit(solution)/shard_map/ppermute | solution.py:368
  2.9 1.8 %collective-permute-start = (bf16[256,256]{1,0:T(8,128)(2,1)S(1)}, bf16[256,256]{1,0:T(8,128)(2,1)S(1)}, u32[]{:S(2)}, u32[]{:S(2)}) collective-permute-start(bf16[256,256]{1,0:T(8,128)(2,1)S(1)} %latent.1.refs_1_), channel_id=1, source_target_pairs={{0,1},{1,0},{2,3},{3,2},{4,5},{5,4},{6,7},{7,6},{8,9},{9,8},{10,11... | collective-permute-start | bytes 393224 | tf_op jit(solution)/shard_map/ppermute | solution.py:369
  6.7 1.4 %prepare.1 = (f32[256,256]{1,0:T(8,128)S(1)}, f32[256,256]{1,0:T(8,128)S(1)}, f32[64,256]{1,0:T(8,128)S(1)}, bf16[64,240]{1,0:T(8,128)(2,1)S(1)}, f32[240,128]{1...) custom-call(f32[1]{0:T(128)S(6)} %copy.12.drift_ref, f32[1]{0:T(128)S(6)} %copy.13.eps_ref, ...), custom_call_target="tpu_custom_call" | custom-call | tf_op jit(solution)/shard_map/prepare/pallas_call | solution.py:350
  8.0 0.0 collective-permute-done.1.refs_2_
  8.1 0.0 collective-permute-done.refs_0_
  8.1 2.7 %first.1 = bf16[832,256]{1,0:T(8,128)(2,1)S(1)} custom-call(bf16[256,256]{1,0:T(8,128)(2,1)S(1)} %collective-permute-done.refs_0_, bf16[256,256]{1,0:T(8,128)(2,1)S(1)} %latent.1.refs_1_, bf16[256,256]{1,0:T(8,128)(2,1)S(1)} %collective-permute-done.1.refs_2_, bf16[64,240]{1,0:T(8,128)(2,1)S(1)} %get-tuple-element.21.refs_3_, ...), custom_call_target="tpu_custom_call" | custom-call | tf_op jit(solution)/shard_map/first/pallas_call | solution.py:350
  10.8 23.8 %all_to_all.10 = bf16[8,104,256]{2,1,0:T(8,128)(2,1)S(1)} all-to-all(bf16[8,104,256]{2,1,0:T(8,128)(2,1)S(1)} %bitcast.18), channel_id=1, replica_groups={{0,8,16,24,32,40,48,56},{64,72,80,88,96,104,112,120},{128,136,144,152,1..., dimensions={0} | all-to-all | bytes 851968 | tf_op jit(solution)/shard_map/all_to_all | solution.py:373
  34.6 0.1 scan.1
  34.7 4.7 %collective-permute-start.4 = (bf16[96,256]{1,0:T(8,128)(2,1)S(1)}, bf16[96,256]{1,0:T(8,128)(2,1)S(1)}, u32[]{:S(2)}, u32[]{:S(2)}) collective-permute-start(bf16[96,256]{1,0:T(8,128)(2,1)S(1)} %get-tuple-element.26), channel_id=1, source_target_pairs={{0,192},{8,200},{16,208},{24,216},{32,224},{40,232},{48,240},{56,2... | collective-permute-start | bytes 147464 | tf_op jit(solution)/shard_map/ppermute | solution.py:377
  39.4 1.3 %collective-permute-start.3 = (bf16[96,256]{1,0:T(8,128)(2,1)S(1)}, bf16[96,256]{1,0:T(8,128)(2,1)S(1)}, u32[]{:S(2)}, u32[]{:S(2)}) collective-permute-start(bf16[96,256]{1,0:T(8,128)(2,1)S(1)} %get-tuple-element.26), channel_id=1, source_target_pairs={{0,128},{8,136},{16,144},{24,152},{32,160},{40,168},{48,176},{56,1... | collective-permute-start | bytes 147464 | tf_op jit(solution)/shard_map/ppermute | solution.py:377
  40.7 2.8 %collective-permute-start.2 = (bf16[96,256]{1,0:T(8,128)(2,1)S(1)}, bf16[96,256]{1,0:T(8,128)(2,1)S(1)}, u32[]{:S(2)}, u32[]{:S(2)}) collective-permute-start(bf16[96,256]{1,0:T(8,128)(2,1)S(1)} %get-tuple-element.26), channel_id=1, source_target_pairs={{0,64},{8,72},{16,80},{24,88},{32,96},{40,104},{48,112},{56,120},{... | collective-permute-start | bytes 147464 | tf_op jit(solution)/shard_map/ppermute | solution.py:377
  43.4 0.0 collective-permute-done.4.three_ref
  43.4 0.0 collective-permute-done.3.two_ref
  43.5 1.7 %collective-permute-done.2.one_ref = bf16[96,256]{1,0:T(8,128)(2,1)S(1)} collective-permute-done((bf16[96,256]{1,0:T(8,128)(2,1)S(1)}, bf16[96,256]{1,0:T(8,128)(2,1)S(1)}, u32[]{:S(2)}, u32[]{:S(2)}) %collective-permute-start.2) | collective-permute-done | bytes 49184 | tf_op jit(solution)/shard_map/ppermute | solution.py:377
  45.2 0.1 state.1
  45.2 1.9 %collective-permute-start.6 = (bf16[512,256]{1,0:T(8,128)(2,1)S(1)}, bf16[512,256]{1,0:T(8,128)(2,1)S(1)}, u32[]{:S(2)}, u32[]{:S(2)}) collective-permute-start(bf16[512,256]{1,0:T(8,128)(2,1)S(1)} %get-tuple-element.28.refs_1_), channel_id=1, source_target_pairs={{1,2},{2,1},{3,4},{4,3},{5,6},{6,5},{9,10},{10,9},{11,12},{12,11},... | collective-permute-start | bytes 786440 | tf_op jit(solution)/shard_map/ppermute | solution.py:368
  47.2 1.5 %collective-permute-start.5 = (bf16[512,256]{1,0:T(8,128)(2,1)S(1)}, bf16[512,256]{1,0:T(8,128)(2,1)S(1)}, u32[]{:S(2)}, u32[]{:S(2)}) collective-permute-start(bf16[512,256]{1,0:T(8,128)(2,1)S(1)} %get-tuple-element.28.refs_1_), channel_id=1, source_target_pairs={{0,1},{1,0},{2,3},{3,2},{4,5},{5,4},{6,7},{7,6},{8,9},{9,8},{10,11... | collective-permute-start | bytes 786440 | tf_op jit(solution)/shard_map/ppermute | solution.py:369
  48.6 0.1 tune.1
  48.7 4.2 %collective-permute-done.6.refs_2_ = bf16[512,256]{1,0:T(8,128)(2,1)S(1)} collective-permute-done((bf16[512,256]{1,0:T(8,128)(2,1)S(1)}, bf16[512,256]{1,0:T(8,128)(2,1)S(1)}, u32[]{:S(2)}, u32[]{:S(2)}) %collective-permute-start.6) | collective-permute-done | bytes 262176 | tf_op jit(solution)/shard_map/ppermute | solution.py:368
  52.9 0.0 collective-permute-done.5.refs_0_
  52.9 3.5 %second.1 = (f32[256,256]{1,0:T(8,128)S(1)}, f32[32,256]{1,0:T(8,128)S(1)}) custom-call(bf16[512,256]{1,0:T(8,128)(2,1)S(1)} %collective-permute-done.5.refs_0_, bf16[512,256]{1,0:T(8,128)(2,1)S(1)} %get-tuple-element.28.refs_1_, bf16[512,256]{1,0:T(8,128)(2,1)S(1)} %collective-permute-done.6.refs_2_, bf16[64,240]{1,0:T(8,128)(2,1)S(1)} %get-tuple-element.30.refs_3_, ...), custom_call_target="tpu_custom_call" | custom-call | tf_op jit(solution)/shard_map/second/pallas_call | solution.py:350
  56.4 3.0 %collective-permute-start.9 = (f32[32,256]{1,0:T(8,128)S(1)}, f32[32,256]{1,0:T(8,128)S(1)}, u32[]{:S(2)}, u32[]{:S(2)}) collective-permute-start(f32[32,256]{1,0:T(8,128)S(1)} %get-tuple-element.33), channel_id=1, source_target_pairs={{0,192},{8,200},{16,208},{24,216},{32,224},{40,232},{48,240},{56,2... | collective-permute-start | bytes 98312 | tf_op jit(solution)/shard_map/ppermute | solution.py:377
  59.4 2.0 %collective-permute-start.8 = (f32[32,256]{1,0:T(8,128)S(1)}, f32[32,256]{1,0:T(8,128)S(1)}, u32[]{:S(2)}, u32[]{:S(2)}) collective-permute-start(f32[32,256]{1,0:T(8,128)S(1)} %get-tuple-element.33), channel_id=1, source_target_pairs={{0,128},{8,136},{16,144},{24,152},{32,160},{40,168},{48,176},{56,1... | collective-permute-start | bytes 98312 | tf_op jit(solution)/shard_map/ppermute | solution.py:377
  61.4 2.1 %collective-permute-start.7 = (f32[32,256]{1,0:T(8,128)S(1)}, f32[32,256]{1,0:T(8,128)S(1)}, u32[]{:S(2)}, u32[]{:S(2)}) collective-permute-start(f32[32,256]{1,0:T(8,128)S(1)} %get-tuple-element.33), channel_id=1, source_target_pairs={{0,64},{8,72},{16,80},{24,88},{32,96},{40,104},{48,112},{56,120},{... | collective-permute-start | bytes 98312 | tf_op jit(solution)/shard_map/ppermute | solution.py:377
  63.5 0.0 collective-permute-done.9.three_ref
  63.5 0.0 collective-permute-done.8.two_ref
  63.5 1.6 %collective-permute-done.7.one_ref = f32[32,256]{1,0:T(8,128)S(1)} collective-permute-done((f32[32,256]{1,0:T(8,128)S(1)}, f32[32,256]{1,0:T(8,128)S(1)}, u32[]{:S(2)}, u32[]{:S(2)}) %collective-permute-start.7) | collective-permute-done | bytes 32800 | tf_op jit(solution)/shard_map/ppermute | solution.py:377
  65.1 13.6 %all_to_all.11 = f32[8,32,256]{2,1,0:T(8,128)S(1)} all-to-all(f32[8,32,256]{2,1,0:T(8,128)S(1)} %bitcast.19), channel_id=1, replica_groups={{0,8,16,24,32,40,48,56},{64,72,80,88,96,104,112,120},{128,136,144,152,1..., dimensions={0} | all-to-all | bytes 524288 | tf_op jit(solution)/shard_map/all_to_all | solution.py:373
  78.6 0.8 final.1
  (1 shorter events, 0.0 us)
Async XLA Ops:
  1.0 7.0 %collective-permute-start.1 = (bf16[256,256]{1,0:T(8,128)(2,1)S(1)}, bf16[256,256]{1,0:T(8,128)(2,1)S(1)}, u32[]{:S(2)}, u32[]{:S(2)}) collective-permute-start(bf16[256,256]{1,0:T(8,128)(2,1)S(1)} %latent.1.refs_1_), channel_id=1, source_target_pairs={{1,2},{2,1},{3,4},{4,3},{5,6},{6,5},{9,10},{10,9},{11,12},{12,11},... | collective-permute-start | bytes 393224 | tf_op jit(solution)/shard_map/ppermute | solution.py:368
  2.9 5.1 %collective-permute-start = (bf16[256,256]{1,0:T(8,128)(2,1)S(1)}, bf16[256,256]{1,0:T(8,128)(2,1)S(1)}, u32[]{:S(2)}, u32[]{:S(2)}) collective-permute-start(bf16[256,256]{1,0:T(8,128)(2,1)S(1)} %latent.1.refs_1_), channel_id=1, source_target_pairs={{0,1},{1,0},{2,3},{3,2},{4,5},{5,4},{6,7},{7,6},{8,9},{9,8},{10,11... | collective-permute-start | bytes 393224 | tf_op jit(solution)/shard_map/ppermute | solution.py:369
  34.7 8.7 %collective-permute-start.4 = (bf16[96,256]{1,0:T(8,128)(2,1)S(1)}, bf16[96,256]{1,0:T(8,128)(2,1)S(1)}, u32[]{:S(2)}, u32[]{:S(2)}) collective-permute-start(bf16[96,256]{1,0:T(8,128)(2,1)S(1)} %get-tuple-element.26), channel_id=1, source_target_pairs={{0,192},{8,200},{16,208},{24,216},{32,224},{40,232},{48,240},{56,2... | collective-permute-start | bytes 147464 | tf_op jit(solution)/shard_map/ppermute | solution.py:377
  39.4 4.1 %collective-permute-start.3 = (bf16[96,256]{1,0:T(8,128)(2,1)S(1)}, bf16[96,256]{1,0:T(8,128)(2,1)S(1)}, u32[]{:S(2)}, u32[]{:S(2)}) collective-permute-start(bf16[96,256]{1,0:T(8,128)(2,1)S(1)} %get-tuple-element.26), channel_id=1, source_target_pairs={{0,128},{8,136},{16,144},{24,152},{32,160},{40,168},{48,176},{56,1... | collective-permute-start | bytes 147464 | tf_op jit(solution)/shard_map/ppermute | solution.py:377
  40.7 4.5 %collective-permute-start.2 = (bf16[96,256]{1,0:T(8,128)(2,1)S(1)}, bf16[96,256]{1,0:T(8,128)(2,1)S(1)}, u32[]{:S(2)}, u32[]{:S(2)}) collective-permute-start(bf16[96,256]{1,0:T(8,128)(2,1)S(1)} %get-tuple-element.26), channel_id=1, source_target_pairs={{0,64},{8,72},{16,80},{24,88},{32,96},{40,104},{48,112},{56,120},{... | collective-permute-start | bytes 147464 | tf_op jit(solution)/shard_map/ppermute | solution.py:377
  45.2 7.7 %collective-permute-start.6 = (bf16[512,256]{1,0:T(8,128)(2,1)S(1)}, bf16[512,256]{1,0:T(8,128)(2,1)S(1)}, u32[]{:S(2)}, u32[]{:S(2)}) collective-permute-start(bf16[512,256]{1,0:T(8,128)(2,1)S(1)} %get-tuple-element.28.refs_1_), channel_id=1, source_target_pairs={{1,2},{2,1},{3,4},{4,3},{5,6},{6,5},{9,10},{10,9},{11,12},{12,11},... | collective-permute-start | bytes 786440 | tf_op jit(solution)/shard_map/ppermute | solution.py:368
  47.2 5.8 %collective-permute-start.5 = (bf16[512,256]{1,0:T(8,128)(2,1)S(1)}, bf16[512,256]{1,0:T(8,128)(2,1)S(1)}, u32[]{:S(2)}, u32[]{:S(2)}) collective-permute-start(bf16[512,256]{1,0:T(8,128)(2,1)S(1)} %get-tuple-element.28.refs_1_), channel_id=1, source_target_pairs={{0,1},{1,0},{2,3},{3,2},{4,5},{5,4},{6,7},{7,6},{8,9},{9,8},{10,11... | collective-permute-start | bytes 786440 | tf_op jit(solution)/shard_map/ppermute | solution.py:369
  56.4 7.1 %collective-permute-start.9 = (f32[32,256]{1,0:T(8,128)S(1)}, f32[32,256]{1,0:T(8,128)S(1)}, u32[]{:S(2)}, u32[]{:S(2)}) collective-permute-start(f32[32,256]{1,0:T(8,128)S(1)} %get-tuple-element.33), channel_id=1, source_target_pairs={{0,192},{8,200},{16,208},{24,216},{32,224},{40,232},{48,240},{56,2... | collective-permute-start | bytes 98312 | tf_op jit(solution)/shard_map/ppermute | solution.py:377
  59.4 4.1 %collective-permute-start.8 = (f32[32,256]{1,0:T(8,128)S(1)}, f32[32,256]{1,0:T(8,128)S(1)}, u32[]{:S(2)}, u32[]{:S(2)}) collective-permute-start(f32[32,256]{1,0:T(8,128)S(1)} %get-tuple-element.33), channel_id=1, source_target_pairs={{0,128},{8,136},{16,144},{24,152},{32,160},{40,168},{48,176},{56,1... | collective-permute-start | bytes 98312 | tf_op jit(solution)/shard_map/ppermute | solution.py:377
  61.4 3.7 %collective-permute-start.7 = (f32[32,256]{1,0:T(8,128)S(1)}, f32[32,256]{1,0:T(8,128)S(1)}, u32[]{:S(2)}, u32[]{:S(2)}) collective-permute-start(f32[32,256]{1,0:T(8,128)S(1)} %get-tuple-element.33), channel_id=1, source_target_pairs={{0,64},{8,72},{16,80},{24,88},{32,96},{40,104},{48,112},{56,120},{... | collective-permute-start | bytes 98312 | tf_op jit(solution)/shard_map/ppermute | solution.py:377

commit v4 on v3

--- a/solution.py
+++ b/solution.py
@@ -35,11 +35,6 @@
     return pieces
 
 
-def latent_kernel(x_ref, out_ref):
-    for plane, block, rows, lanes in tiles():
-        out_ref[rows, lanes] = swapped(x_ref, plane, block).astype(BF)
-
-
 def stacked_kernel(pieces, pads):
     rows = []
     for kh in range(3):
@@ -52,35 +47,34 @@
     return jnp.concatenate([stacked, spare], axis=0).T[:HID, : 3 * TAPS].astype(BF)
 
 
-def prepare_kernel(
-    drift_ref, eps_ref, scale_ref, x_ref, noise_ref, first_ref, w_in_ref, bias_in_ref, level_bias_ref, w_out_ref, bias_out_ref,
-    base_ref, fresh_ref, start_ref, kernel_in_ref, spread_ref, kernel_out_ref, params_ref, first,
+def opening_kernel(
+    x_ref, noise_ref, first_ref, w_in_ref, bias_in_ref, level_bias_ref, w_out_ref, bias_out_ref,
+    latent_ref, state_ref, noise_out_ref, start_ref, kernel_in_ref, spread_ref, kernel_out_ref, biases_ref, column_ref,
+    first,
 ):
-    same = lax.broadcasted_iota(jnp.int32, (C, C), 0) == lax.broadcasted_iota(jnp.int32, (C, C), 1)
-    drift, eps, scale = (jnp.full((1, W), ref[0], F32) for ref in (drift_ref, eps_ref, scale_ref))
-    column = jnp.sum(jnp.where(same, jnp.broadcast_to(bias_out_ref[...], (C, C)), 0.0), axis=1, keepdims=True)
-    shift = jnp.concatenate([eps * jnp.broadcast_to(column, (C, W))] * 8, axis=0)
     edge = jnp.zeros((2 * C, LANES), F32)
     first[: 2 * C, :] = edge
     first[2 * C + H * C :, :] = edge
     for plane, block, rows, lanes in tiles():
-        fresh = scale * swapped(noise_ref, plane, block) + shift
-        fresh_ref[rows, lanes] = fresh
-        base_ref[rows, lanes] = drift * swapped(x_ref, plane, block) + fresh
+        state = swapped(x_ref, plane, block)
+        state_ref[rows, lanes] = state
+        latent_ref[rows, lanes] = state.astype(BF)
+        noise_out_ref[rows, lanes] = swapped(noise_ref, plane, block)
         first[rows.start + 2 * C : rows.stop + 2 * C, lanes] = swapped(first_ref, plane, block)
     own = pl.multiple_of(lax.axis_index("level") % GROUP * KEEP, KEEP)
     start_ref[...] = first[pl.ds(own, EDGE), :]
 
+    same = lax.broadcasted_iota(jnp.int32, (C, C), 0) == lax.broadcasted_iota(jnp.int32, (C, C), 1)
+    column = jnp.sum(jnp.where(same, jnp.broadcast_to(bias_out_ref[...], (C, C)), 0.0), axis=1, keepdims=True)
+    column_ref[...] = jnp.broadcast_to(column, (C, W))
     bias = 0.5 * (bias_in_ref[...] + level_bias_ref[...])
-    bias = jnp.concatenate([bias, jnp.zeros((1, W - HID), F32)], axis=1)
-    rows = split(bias, 3)
+    biases = split(jnp.concatenate([bias, jnp.zeros((1, W - HID), F32)], axis=1), 3)
     index = lax.broadcasted_iota(jnp.int32, (C, W), 0)
-    left = right = jnp.zeros((C, W), F32)
-    for k, row in enumerate(rows + split(drift, 3)):
-        left = jnp.where(index == k, row, left)
-    for k, row in enumerate(split(eps, 3)):
-        right = jnp.where(index == 3 + k, row, right)
-    params_ref[...] = jnp.concatenate([left, right], axis=1).astype(BF)
+    nothing = jnp.zeros((C, W), F32)
+    table = nothing
+    for k, row in enumerate(biases):
+        table = jnp.where(index == k, row, table)
+    biases_ref[...] = table
 
     wide = jnp.zeros((C, W - HID), F32)
     pieces = [
@@ -91,15 +85,33 @@
         ]
         for kh in range(3)
     ]
-    nothing = jnp.zeros((C, W), F32)
-    top = lax.broadcasted_iota(jnp.int32, (C, W), 0) == 0
     spread_ref[...] = stacked_kernel(pieces, [nothing] * 3)
-    kernel_in_ref[...] = turned(stacked_kernel(pieces, [jnp.where(top, rows[kh], 0.0) for kh in range(3)]))
+    kernel_in_ref[...] = turned(stacked_kernel(pieces, [jnp.where(index == 0, row, 0.0) for row in biases]))
     rows_of = [
         jnp.concatenate([w_out_ref[kd * 9 + kh * 3 + kw].astype(F32) for kd in range(3) for kw in range(3)], axis=0)
         for kh in range(3)
     ]
     kernel_out_ref[...] = jnp.concatenate(rows_of, axis=1).astype(BF)
+
+
+def prepare_kernel(
+    drift_ref, eps_ref, scale_ref, state_ref, noise_ref, biases_ref, column_ref, base_ref, fresh_ref, params_ref
+):
+    drift, eps, scale = (jnp.full((1, W), ref[0], F32) for ref in (drift_ref, eps_ref, scale_ref))
+    column = eps * column_ref[...]
+    shift = jnp.concatenate([column, column], axis=1)
+    for row in range(H):
+        rows = slice(row * C, row * C + C)
+        fresh = scale_ref[0] * noise_ref[rows, :] + shift
+        fresh_ref[rows, :] = fresh
+        base_ref[rows, :] = drift_ref[0] * state_ref[rows, :] + fresh
+    index = lax.broadcasted_iota(jnp.int32, (C, W), 0)
+    left, right = biases_ref[...], jnp.zeros((C, W), F32)
+    for k, row in enumerate(split(drift, 3)):
+        left = jnp.where(index == 3 + k, row, left)
+    for k, row in enumerate(split(eps, 3)):
+        right = jnp.where(index == 3 + k, row, right)
+    params_ref[...] = jnp.concatenate([left, right], axis=1).astype(BF)
 
 
 def edge_masks():
@@ -377,21 +389,25 @@
             lax.ppermute(total, "level", [(i, i + k) for i in range(levels - k)]) for k in range(GROUP, levels, GROUP)
         ]
 
-    latent = call(latent_kernel, (trajectory[0],), [pltpu.VMEM((H * C, LANES), BF)], name="latent")
-    base, fresh, start, kernel_in, spread, kernel_out, params = call(
-        prepare_kernel,
+    latent, first_state, noise, start, kernel_in, spread, kernel_out, biases, column = call(
+        opening_kernel,
         (
-            drift, eps, scale,
             trajectory[0], noise_draw[0], first_latent,
             jnp.transpose(w_in, (2, 3, 4, 1, 0)).reshape(27, C, HID), bias_in[None], level_bias,
             jnp.transpose(w_out, (2, 3, 4, 0, 1)).reshape(27, C, HID), bias_out[None],
         ),
         [
-            pltpu.VMEM((H * C, LANES), F32), pltpu.VMEM((H * C, LANES), F32), pltpu.VMEM((EDGE, LANES), F32),
-            pltpu.VMEM((HID, 3 * TAPS), BF),
-            pltpu.VMEM((3 * TAPS, W), F32), pltpu.VMEM((9 * C, 3 * HID), BF), pltpu.VMEM((C, LANES), BF),
+            pltpu.VMEM((H * C, LANES), BF), pltpu.VMEM((H * C, LANES), F32), pltpu.VMEM((H * C, LANES), F32),
+            pltpu.VMEM((EDGE, LANES), F32), pltpu.VMEM((HID, 3 * TAPS), BF), pltpu.VMEM((3 * TAPS, W), F32),
+            pltpu.VMEM((9 * C, 3 * HID), BF), pltpu.VMEM((C, W), F32), pltpu.VMEM((C, W), F32),
         ],
         [pltpu.VMEM(((H + 4) * C, LANES), F32)],
+        name="opening",
+    )
+    base, fresh, params = call(
+        prepare_kernel,
+        (drift, eps, scale, *near(first_state, noise, biases, column)),
+        [pltpu.VMEM((H * C, LANES), F32), pltpu.VMEM((H * C, LANES), F32), pltpu.VMEM((C, LANES), BF)],
         name="prepare",
         scalars=3,
     )

time: 80.3 us -> 80.2 us (level)
  Pallas kernels: 9.6 us -> 8.67 us
    pallas_call x9, Pallas kernels: 9.6 us -> 8.67 us  [call(): pl.pallas_call(kernel, out_shape=outs if len(outs) > 1 else outs[0], in_s...]
  transfers between devices with their start and end apart: 10 -> 10, of which waited for: 3 -> 4; matrix products, arithmetic and copies ran while one was open for 0% -> 0% of each run, Pallas kernels for 2% -> 0%
where the time goes in v4:
time: 80.2 us; the launch traced here: 79.3 us
  blocking collectives  37.6 us (47%)
  starting transfers between devices  23.1 us (29%)
  Pallas kernels  8.67 us (11%)
  waiting for transfers between devices  7.78 us (10%)
  between operations  2.08 us (3%)
    all_to_all x2, blocking collectives, exchange(): lax.all_to_all(parts, 'level', 0, 0, axis_index_groups=groups)  37.6 us
    ppermute x6, starting transfers between devices, earlier_groups(): lax.ppermute(total, 'level', [(i, i + k) for i in range(levels - k)])  15.8 us
    pallas_call x9, Pallas kernels, call(): pl.pallas_call(kernel, out_shape=outs if len(outs) > 1 else outs[0], in_s...  8.67 us
    ppermute x2, waiting for transfers between devices, neighbours(): crossed = lax.ppermute(latent, 'slab', crossings)  4.5 us
    ppermute x2, starting transfers between devices, neighbours(): crossed = lax.ppermute(latent, 'slab', crossings)  3.84 us
    ppermute x2, starting transfers between devices, neighbours(): return (lax.ppermute(latent, 'slab', pairs), latent, crossed)  3.53 us
    ppermute x6, waiting for transfers between devices, earlier_groups(): lax.ppermute(total, 'level', [(i, i + k) for i in range(levels - k)])  3.28 us
  transfers between devices with their start and end apart: 10, of which 4 were waited for; matrix products, arithmetic and copies ran while one was open for 0% of the time, Pallas kernels for 0%

profile of v4, /device:TPU:8, one launch (start us, length us, event | category | flops | bytes accessed | tf_op | source)
XLA Modules:
  0.0 79.3 jit_solution(15539111547629040192)
XLA Ops:
  0.0 1.4 %opening.1 = (bf16[256,256]{1,0:T(8,128)(2,1)S(1)}, f32[256,256]{1,0:T(8,128)S(1)}, f32[256,256]{1,0:T(8,128)S(1)}, f32[64,256]{1,0:T(8,128)S(1)}, bf16[64,240]{...) custom-call(f32[8,2,32,128]{3,2,1,0:T(8,128)} %bitcast.21, ...), custom_call_target="tpu_custom_call" | custom-call | tf_op jit(solution)/shard_map/opening/pallas_call | solution.py:362
  1.4 1.9 %collective-permute-start.1 = (bf16[256,256]{1,0:T(8,128)(2,1)S(1)}, bf16[256,256]{1,0:T(8,128)(2,1)S(1)}, u32[]{:S(2)}, u32[]{:S(2)}) collective-permute-start(bf16[256,256]{1,0:T(8,128)(2,1)S(1)} %get-tuple-element.26.refs_1_), channel_id=1, source_target_pairs={{1,2},{2,1},{3,4},{4,3},{5,6},{6,5},{9,10},{10,9},{11,12},{12,11},... | collective-permute-start | bytes 393224 | tf_op jit(solution)/shard_map/ppermute | solution.py:380
  3.4 1.8 %collective-permute-start = (bf16[256,256]{1,0:T(8,128)(2,1)S(1)}, bf16[256,256]{1,0:T(8,128)(2,1)S(1)}, u32[]{:S(2)}, u32[]{:S(2)}) collective-permute-start(bf16[256,256]{1,0:T(8,128)(2,1)S(1)} %get-tuple-element.26.refs_1_), channel_id=1, source_target_pairs={{0,1},{1,0},{2,3},{3,2},{4,5},{5,4},{6,7},{7,6},{8,9},{9,8},{10,11... | collective-permute-start | bytes 393224 | tf_op jit(solution)/shard_map/ppermute | solution.py:381
  7.1 0.1 prepare.1
  7.1 0.6 collective-permute-done.1.refs_2_
  7.7 0.0 collective-permute-done.refs_0_
  7.7 2.7 %first.1 = bf16[832,256]{1,0:T(8,128)(2,1)S(1)} custom-call(bf16[256,256]{1,0:T(8,128)(2,1)S(1)} %collective-permute-done.refs_0_, bf16[256,256]{1,0:T(8,128)(2,1)S(1)} %get-tuple-element.26.refs_1_, bf16[256,256]{1,0:T(8,128)(2,1)S(1)} %collective-permute-done.1.refs_2_, bf16[64,240]{1,0:T(8,128)(2,1)S(1)} %get-tuple-element.27.refs_3_, ...), custom_call_target="tpu_custom_call" | custom-call | tf_op jit(solution)/shard_map/first/pallas_call | solution.py:362
  10.5 23.9 %all_to_all.10 = bf16[8,104,256]{2,1,0:T(8,128)(2,1)S(1)} all-to-all(bf16[8,104,256]{2,1,0:T(8,128)(2,1)S(1)} %bitcast.18), channel_id=1, replica_groups={{0,8,16,24,32,40,48,56},{64,72,80,88,96,104,112,120},{128,136,144,152,1..., dimensions={0} | all-to-all | bytes 851968 | tf_op jit(solution)/shard_map/all_to_all | solution.py:385
  34.4 0.1 scan.1
  34.5 4.7 %collective-permute-start.4 = (bf16[96,256]{1,0:T(8,128)(2,1)S(1)}, bf16[96,256]{1,0:T(8,128)(2,1)S(1)}, u32[]{:S(2)}, u32[]{:S(2)}) collective-permute-start(bf16[96,256]{1,0:T(8,128)(2,1)S(1)} %get-tuple-element.36), channel_id=1, source_target_pairs={{0,192},{8,200},{16,208},{24,216},{32,224},{40,232},{48,240},{56,2... | collective-permute-start | bytes 147464 | tf_op jit(solution)/shard_map/ppermute | solution.py:389
  39.1 1.3 %collective-permute-start.3 = (bf16[96,256]{1,0:T(8,128)(2,1)S(1)}, bf16[96,256]{1,0:T(8,128)(2,1)S(1)}, u32[]{:S(2)}, u32[]{:S(2)}) collective-permute-start(bf16[96,256]{1,0:T(8,128)(2,1)S(1)} %get-tuple-element.36), channel_id=1, source_target_pairs={{0,128},{8,136},{16,144},{24,152},{32,160},{40,168},{48,176},{56,1... | collective-permute-start | bytes 147464 | tf_op jit(solution)/shard_map/ppermute | solution.py:389
  40.4 2.8 %collective-permute-start.2 = (bf16[96,256]{1,0:T(8,128)(2,1)S(1)}, bf16[96,256]{1,0:T(8,128)(2,1)S(1)}, u32[]{:S(2)}, u32[]{:S(2)}) collective-permute-start(bf16[96,256]{1,0:T(8,128)(2,1)S(1)} %get-tuple-element.36), channel_id=1, source_target_pairs={{0,64},{8,72},{16,80},{24,88},{32,96},{40,104},{48,112},{56,120},{... | collective-permute-start | bytes 147464 | tf_op jit(solution)/shard_map/ppermute | solution.py:389
  43.2 0.0 collective-permute-done.4.three_ref
  43.2 0.0 collective-permute-done.3.two_ref
  43.2 1.7 %collective-permute-done.2.one_ref = bf16[96,256]{1,0:T(8,128)(2,1)S(1)} collective-permute-done((bf16[96,256]{1,0:T(8,128)(2,1)S(1)}, bf16[96,256]{1,0:T(8,128)(2,1)S(1)}, u32[]{:S(2)}, u32[]{:S(2)}) %collective-permute-start.2) | collective-permute-done | bytes 49184 | tf_op jit(solution)/shard_map/ppermute | solution.py:389
  44.9 0.1 state.1
  45.0 1.9 %collective-permute-start.6 = (bf16[512,256]{1,0:T(8,128)(2,1)S(1)}, bf16[512,256]{1,0:T(8,128)(2,1)S(1)}, u32[]{:S(2)}, u32[]{:S(2)}) collective-permute-start(bf16[512,256]{1,0:T(8,128)(2,1)S(1)} %get-tuple-element.38.refs_1_), channel_id=1, source_target_pairs={{1,2},{2,1},{3,4},{4,3},{5,6},{6,5},{9,10},{10,9},{11,12},{12,11},... | collective-permute-start | bytes 786440 | tf_op jit(solution)/shard_map/ppermute | solution.py:380
  46.9 1.8 %collective-permute-start.5 = (bf16[512,256]{1,0:T(8,128)(2,1)S(1)}, bf16[512,256]{1,0:T(8,128)(2,1)S(1)}, u32[]{:S(2)}, u32[]{:S(2)}) collective-permute-start(bf16[512,256]{1,0:T(8,128)(2,1)S(1)} %get-tuple-element.38.refs_1_), channel_id=1, source_target_pairs={{0,1},{1,0},{2,3},{3,2},{4,5},{5,4},{6,7},{7,6},{8,9},{9,8},{10,11... | collective-permute-start | bytes 786440 | tf_op jit(solution)/shard_map/ppermute | solution.py:381
  48.7 0.1 tune.1
  48.8 3.9 %collective-permute-done.6.refs_2_ = bf16[512,256]{1,0:T(8,128)(2,1)S(1)} collective-permute-done((bf16[512,256]{1,0:T(8,128)(2,1)S(1)}, bf16[512,256]{1,0:T(8,128)(2,1)S(1)}, u32[]{:S(2)}, u32[]{:S(2)}) %collective-permute-start.6) | collective-permute-done | bytes 262176 | tf_op jit(solution)/shard_map/ppermute | solution.py:380
  52.7 0.0 collective-permute-done.5.refs_0_
  52.7 3.5 %second.1 = (f32[256,256]{1,0:T(8,128)S(1)}, f32[32,256]{1,0:T(8,128)S(1)}) custom-call(bf16[512,256]{1,0:T(8,128)(2,1)S(1)} %collective-permute-done.5.refs_0_, bf16[512,256]{1,0:T(8,128)(2,1)S(1)} %get-tuple-element.38.refs_1_, bf16[512,256]{1,0:T(8,128)(2,1)S(1)} %collective-permute-done.6.refs_2_, bf16[64,240]{1,0:T(8,128)(2,1)S(1)} %get-tuple-element.40.refs_3_, ...), custom_call_target="tpu_custom_call" | custom-call | tf_op jit(solution)/shard_map/second/pallas_call | solution.py:362
  56.2 3.0 %collective-permute-start.9 = (f32[32,256]{1,0:T(8,128)S(1)}, f32[32,256]{1,0:T(8,128)S(1)}, u32[]{:S(2)}, u32[]{:S(2)}) collective-permute-start(f32[32,256]{1,0:T(8,128)S(1)} %get-tuple-element.43), channel_id=1, source_target_pairs={{0,192},{8,200},{16,208},{24,216},{32,224},{40,232},{48,240},{56,2... | collective-permute-start | bytes 98312 | tf_op jit(solution)/shard_map/ppermute | solution.py:389
  59.2 2.0 %collective-permute-start.8 = (f32[32,256]{1,0:T(8,128)S(1)}, f32[32,256]{1,0:T(8,128)S(1)}, u32[]{:S(2)}, u32[]{:S(2)}) collective-permute-start(f32[32,256]{1,0:T(8,128)S(1)} %get-tuple-element.43), channel_id=1, source_target_pairs={{0,128},{8,136},{16,144},{24,152},{32,160},{40,168},{48,176},{56,1... | collective-permute-start | bytes 98312 | tf_op jit(solution)/shard_map/ppermute | solution.py:389
  61.1 2.1 %collective-permute-start.7 = (f32[32,256]{1,0:T(8,128)S(1)}, f32[32,256]{1,0:T(8,128)S(1)}, u32[]{:S(2)}, u32[]{:S(2)}) collective-permute-start(f32[32,256]{1,0:T(8,128)S(1)} %get-tuple-element.43), channel_id=1, source_target_pairs={{0,64},{8,72},{16,80},{24,88},{32,96},{40,104},{48,112},{56,120},{... | collective-permute-start | bytes 98312 | tf_op jit(solution)/shard_map/ppermute | solution.py:389
  63.2 0.0 collective-permute-done.9.three_ref
  63.2 0.0 collective-permute-done.8.two_ref
  63.2 1.6 %collective-permute-done.7.one_ref = f32[32,256]{1,0:T(8,128)S(1)} collective-permute-done((f32[32,256]{1,0:T(8,128)S(1)}, f32[32,256]{1,0:T(8,128)S(1)}, u32[]{:S(2)}, u32[]{:S(2)}) %collective-permute-start.7) | collective-permute-done | bytes 32800 | tf_op jit(solution)/shard_map/ppermute | solution.py:389
  64.8 13.7 %all_to_all.11 = f32[8,32,256]{2,1,0:T(8,128)S(1)} all-to-all(f32[8,32,256]{2,1,0:T(8,128)S(1)} %bitcast.19), channel_id=1, replica_groups={{0,8,16,24,32,40,48,56},{64,72,80,88,96,104,112,120},{128,136,144,152,1..., dimensions={0} | all-to-all | bytes 524288 | tf_op jit(solution)/shard_map/all_to_all | solution.py:385
  78.5 0.8 final.1
  (1 shorter events, 0.0 us)
Async XLA Ops:
  1.4 6.3 %collective-permute-start.1 = (bf16[256,256]{1,0:T(8,128)(2,1)S(1)}, bf16[256,256]{1,0:T(8,128)(2,1)S(1)}, u32[]{:S(2)}, u32[]{:S(2)}) collective-permute-start(bf16[256,256]{1,0:T(8,128)(2,1)S(1)} %get-tuple-element.26.refs_1_), channel_id=1, source_target_pairs={{1,2},{2,1},{3,4},{4,3},{5,6},{6,5},{9,10},{10,9},{11,12},{12,11},... | collective-permute-start | bytes 393224 | tf_op jit(solution)/shard_map/ppermute | solution.py:380
  3.4 4.4 %collective-permute-start = (bf16[256,256]{1,0:T(8,128)(2,1)S(1)}, bf16[256,256]{1,0:T(8,128)(2,1)S(1)}, u32[]{:S(2)}, u32[]{:S(2)}) collective-permute-start(bf16[256,256]{1,0:T(8,128)(2,1)S(1)} %get-tuple-element.26.refs_1_), channel_id=1, source_target_pairs={{0,1},{1,0},{2,3},{3,2},{4,5},{5,4},{6,7},{7,6},{8,9},{9,8},{10,11... | collective-permute-start | bytes 393224 | tf_op jit(solution)/shard_map/ppermute | solution.py:381
  34.5 8.7 %collective-permute-start.4 = (bf16[96,256]{1,0:T(8,128)(2,1)S(1)}, bf16[96,256]{1,0:T(8,128)(2,1)S(1)}, u32[]{:S(2)}, u32[]{:S(2)}) collective-permute-start(bf16[96,256]{1,0:T(8,128)(2,1)S(1)} %get-tuple-element.36), channel_id=1, source_target_pairs={{0,192},{8,200},{16,208},{24,216},{32,224},{40,232},{48,240},{56,2... | collective-permute-start | bytes 147464 | tf_op jit(solution)/shard_map/ppermute | solution.py:389
  39.1 4.1 %collective-permute-start.3 = (bf16[96,256]{1,0:T(8,128)(2,1)S(1)}, bf16[96,256]{1,0:T(8,128)(2,1)S(1)}, u32[]{:S(2)}, u32[]{:S(2)}) collective-permute-start(bf16[96,256]{1,0:T(8,128)(2,1)S(1)} %get-tuple-element.36), channel_id=1, source_target_pairs={{0,128},{8,136},{16,144},{24,152},{32,160},{40,168},{48,176},{56,1... | collective-permute-start | bytes 147464 | tf_op jit(solution)/shard_map/ppermute | solution.py:389
  40.4 4.5 %collective-permute-start.2 = (bf16[96,256]{1,0:T(8,128)(2,1)S(1)}, bf16[96,256]{1,0:T(8,128)(2,1)S(1)}, u32[]{:S(2)}, u32[]{:S(2)}) collective-permute-start(bf16[96,256]{1,0:T(8,128)(2,1)S(1)} %get-tuple-element.36), channel_id=1, source_target_pairs={{0,64},{8,72},{16,80},{24,88},{32,96},{40,104},{48,112},{56,120},{... | collective-permute-start | bytes 147464 | tf_op jit(solution)/shard_map/ppermute | solution.py:389
  45.0 7.7 %collective-permute-start.6 = (bf16[512,256]{1,0:T(8,128)(2,1)S(1)}, bf16[512,256]{1,0:T(8,128)(2,1)S(1)}, u32[]{:S(2)}, u32[]{:S(2)}) collective-permute-start(bf16[512,256]{1,0:T(8,128)(2,1)S(1)} %get-tuple-element.38.refs_1_), channel_id=1, source_target_pairs={{1,2},{2,1},{3,4},{4,3},{5,6},{6,5},{9,10},{10,9},{11,12},{12,11},... | collective-permute-start | bytes 786440 | tf_op jit(solution)/shard_map/ppermute | solution.py:380
  46.9 5.8 %collective-permute-start.5 = (bf16[512,256]{1,0:T(8,128)(2,1)S(1)}, bf16[512,256]{1,0:T(8,128)(2,1)S(1)}, u32[]{:S(2)}, u32[]{:S(2)}) collective-permute-start(bf16[512,256]{1,0:T(8,128)(2,1)S(1)} %get-tuple-element.38.refs_1_), channel_id=1, source_target_pairs={{0,1},{1,0},{2,3},{3,2},{4,5},{5,4},{6,7},{7,6},{8,9},{9,8},{10,11... | collective-permute-start | bytes 786440 | tf_op jit(solution)/shard_map/ppermute | solution.py:381
  56.2 7.1 %collective-permute-start.9 = (f32[32,256]{1,0:T(8,128)S(1)}, f32[32,256]{1,0:T(8,128)S(1)}, u32[]{:S(2)}, u32[]{:S(2)}) collective-permute-start(f32[32,256]{1,0:T(8,128)S(1)} %get-tuple-element.43), channel_id=1, source_target_pairs={{0,192},{8,200},{16,208},{24,216},{32,224},{40,232},{48,240},{56,2... | collective-permute-start | bytes 98312 | tf_op jit(solution)/shard_map/ppermute | solution.py:389
  59.2 4.1 %collective-permute-start.8 = (f32[32,256]{1,0:T(8,128)S(1)}, f32[32,256]{1,0:T(8,128)S(1)}, u32[]{:S(2)}, u32[]{:S(2)}) collective-permute-start(f32[32,256]{1,0:T(8,128)S(1)} %get-tuple-element.43), channel_id=1, source_target_pairs={{0,128},{8,136},{16,144},{24,152},{32,160},{40,168},{48,176},{56,1... | collective-permute-start | bytes 98312 | tf_op jit(solution)/shard_map/ppermute | solution.py:389
  61.1 3.7 %collective-permute-start.7 = (f32[32,256]{1,0:T(8,128)S(1)}, f32[32,256]{1,0:T(8,128)S(1)}, u32[]{:S(2)}, u32[]{:S(2)}) collective-permute-start(f32[32,256]{1,0:T(8,128)S(1)} %get-tuple-element.43), channel_id=1, source_target_pairs={{0,64},{8,72},{16,80},{24,88},{32,96},{40,104},{48,112},{56,120},{... | collective-permute-start | bytes 98312 | tf_op jit(solution)/shard_map/ppermute | solution.py:389

commit v5 on v4

--- a/solution.py
+++ b/solution.py
@@ -254,14 +254,16 @@
 
 
 def state_kernel(start_ref, one_ref, two_ref, three_ref, before_ref, state_ref, latent_ref):
+    group = lax.axis_index("level") // GROUP
     for block in range(EXT // 2):
         rows = slice(block * 16, block * 16 + 16)
         low = rows.start - 2 * C
         offset = start_ref[rows, :]
-        for ref in (one_ref, two_ref, three_ref):
-            offset = offset + ref[rows, :].astype(F32)
+        for k, ref in enumerate((one_ref, two_ref, three_ref)):
+            total = ref[rows, :].astype(F32)
             if 0 <= low < KEEP:
-                offset = offset + ref[EDGE + low : EDGE + low + 16, :].astype(F32)
+                total = total + ref[EDGE + low : EDGE + low + 16, :].astype(F32)
+            offset = offset + jnp.where(group > k, total, 0.0)
         for k in range(GROUP):
             at = slice(k * EDGE + rows.start, k * EDGE + rows.stop)
             state = offset + before_ref[at, :]
@@ -339,7 +341,9 @@
 
 
 def add_kernel(start_ref, one_ref, two_ref, three_ref, sum_ref, out_ref):
-    offset = start_ref[2 * C : 2 * C + KEEP, :] + (one_ref[...] + two_ref[...] + three_ref[...])
+    group = lax.axis_index("level") // GROUP
+    refs = (one_ref, two_ref, three_ref)
+    offset = start_ref[2 * C : 2 * C + KEEP, :] + sum(jnp.where(group > k, ref[...], 0.0) for k, ref in enumerate(refs))
     for k in range(GROUP):
         rows = slice(k * KEEP, k * KEEP + KEEP)
         out_ref[rows, :] = offset + sum_ref[rows, :]
@@ -386,7 +390,8 @@
 
     def earlier_groups(total):
         return [
-            lax.ppermute(total, "level", [(i, i + k) for i in range(levels - k)]) for k in range(GROUP, levels, GROUP)
+            lax.ppermute(total, "level", [(i, (i + k) % levels) for i in range(levels)])
+            for k in range(GROUP, levels, GROUP)
         ]
 
     latent, first_state, noise, start, kernel_in, spread, kernel_out, biases, column = call(

time: 80.2 us -> 76.5 us (0.954)
  starting transfers between devices: 23.1 us -> 14.9 us
  waiting for transfers between devices: 7.78 us -> 12.9 us
    ppermute x6, starting transfers between devices: 15.8 us -> 7.5 us  [earlier_groups(): lax.ppermute(total, 'level', [(i, (i + k) % levels) for i in range(levels)])]
    ppermute x6, waiting for transfers between devices: 3.28 us -> 8.36 us  [earlier_groups(): lax.ppermute(total, 'level', [(i, (i + k) % levels) for i in range(levels)])]
  transfers between devices with their start and end apart: 10 -> 10, of which waited for: 4 -> 8; matrix products, arithmetic and copies ran while one was open for 0% -> 0% of each run, Pallas kernels for 0% -> 0%
where the time goes in v5:
time: 76.5 us; the launch traced here: 75.9 us
  blocking collectives  37.5 us (49%)
  starting transfers between devices  14.9 us (19%)
  waiting for transfers between devices  12.9 us (17%)
  Pallas kernels  8.68 us (11%)
  between operations  2.01 us (3%)
    all_to_all x2, blocking collectives, exchange(): lax.all_to_all(parts, 'level', 0, 0, axis_index_groups=groups)  37.5 us
    pallas_call x9, Pallas kernels, call(): pl.pallas_call(kernel, out_shape=outs if len(outs) > 1 else outs[0], in_s...  8.68 us
    ppermute x6, waiting for transfers between devices, earlier_groups(): lax.ppermute(total, 'level', [(i, (i + k) % levels) for i in range(levels)])  8.36 us
    ppermute x6, starting transfers between devices, earlier_groups(): lax.ppermute(total, 'level', [(i, (i + k) % levels) for i in range(levels)])  7.5 us
    ppermute x2, waiting for transfers between devices, neighbours(): crossed = lax.ppermute(latent, 'slab', crossings)  4.5 us
    ppermute x2, starting transfers between devices, neighbours(): crossed = lax.ppermute(latent, 'slab', crossings)  3.84 us
    ppermute x2, starting transfers between devices, neighbours(): return (lax.ppermute(latent, 'slab', pairs), latent, crossed)  3.53 us
  transfers between devices with their start and end apart: 10, of which 8 were waited for; matrix products, arithmetic and copies ran while one was open for 0% of the time, Pallas kernels for 0%

profile of v5, /device:TPU:8, one launch (start us, length us, event | category | flops | bytes accessed | tf_op | source)
XLA Modules:
  0.0 75.9 jit_solution(5245411446496203114)
XLA Ops:
  0.0 1.4 %opening.1 = (bf16[256,256]{1,0:T(8,128)(2,1)S(1)}, f32[256,256]{1,0:T(8,128)S(1)}, f32[256,256]{1,0:T(8,128)S(1)}, f32[64,256]{1,0:T(8,128)S(1)}, bf16[64,240]{...) custom-call(f32[8,2,32,128]{3,2,1,0:T(8,128)} %bitcast.21, ...), custom_call_target="tpu_custom_call" | custom-call | tf_op jit(solution)/shard_map/opening/pallas_call | solution.py:366
  1.4 1.9 %collective-permute-start.1 = (bf16[256,256]{1,0:T(8,128)(2,1)S(1)}, bf16[256,256]{1,0:T(8,128)(2,1)S(1)}, u32[]{:S(2)}, u32[]{:S(2)}) collective-permute-start(bf16[256,256]{1,0:T(8,128)(2,1)S(1)} %get-tuple-element.26.refs_1_), channel_id=1, source_target_pairs={{1,2},{2,1},{3,4},{4,3},{5,6},{6,5},{9,10},{10,9},{11,12},{12,11},... | collective-permute-start | bytes 393224 | tf_op jit(solution)/shard_map/ppermute | solution.py:384
  3.4 1.8 %collective-permute-start = (bf16[256,256]{1,0:T(8,128)(2,1)S(1)}, bf16[256,256]{1,0:T(8,128)(2,1)S(1)}, u32[]{:S(2)}, u32[]{:S(2)}) collective-permute-start(bf16[256,256]{1,0:T(8,128)(2,1)S(1)} %get-tuple-element.26.refs_1_), channel_id=1, source_target_pairs={{0,1},{1,0},{2,3},{3,2},{4,5},{5,4},{6,7},{7,6},{8,9},{9,8},{10,11... | collective-permute-start | bytes 393224 | tf_op jit(solution)/shard_map/ppermute | solution.py:385
  7.1 0.1 prepare.1
  7.1 0.6 collective-permute-done.1.refs_2_
  7.7 0.0 collective-permute-done.refs_0_
  7.7 2.7 %first.1 = bf16[832,256]{1,0:T(8,128)(2,1)S(1)} custom-call(bf16[256,256]{1,0:T(8,128)(2,1)S(1)} %collective-permute-done.refs_0_, bf16[256,256]{1,0:T(8,128)(2,1)S(1)} %get-tuple-element.26.refs_1_, bf16[256,256]{1,0:T(8,128)(2,1)S(1)} %collective-permute-done.1.refs_2_, bf16[64,240]{1,0:T(8,128)(2,1)S(1)} %get-tuple-element.27.refs_3_, ...), custom_call_target="tpu_custom_call" | custom-call | tf_op jit(solution)/shard_map/first/pallas_call | solution.py:366
  10.5 23.9 %all_to_all.10 = bf16[8,104,256]{2,1,0:T(8,128)(2,1)S(1)} all-to-all(bf16[8,104,256]{2,1,0:T(8,128)(2,1)S(1)} %bitcast.18), channel_id=1, replica_groups={{0,8,16,24,32,40,48,56},{64,72,80,88,96,104,112,120},{128,136,144,152,1..., dimensions={0} | all-to-all | bytes 851968 | tf_op jit(solution)/shard_map/all_to_all | solution.py:389
  34.4 0.1 scan.1
  34.5 2.8 %collective-permute-start.4 = (bf16[96,256]{1,0:T(8,128)(2,1)S(1)}, bf16[96,256]{1,0:T(8,128)(2,1)S(1)}, u32[]{:S(2)}, u32[]{:S(2)}) collective-permute-start(bf16[96,256]{1,0:T(8,128)(2,1)S(1)} %get-tuple-element.36), channel_id=1, source_target_pairs={{0,192},{8,200},{16,208},{24,216},{32,224},{40,232},{48,240},{56,2... | collective-permute-start | bytes 147464 | tf_op jit(solution)/shard_map/ppermute | solution.py:393
  37.3 0.8 %collective-permute-start.3 = (bf16[96,256]{1,0:T(8,128)(2,1)S(1)}, bf16[96,256]{1,0:T(8,128)(2,1)S(1)}, u32[]{:S(2)}, u32[]{:S(2)}) collective-permute-start(bf16[96,256]{1,0:T(8,128)(2,1)S(1)} %get-tuple-element.36), channel_id=1, source_target_pairs={{0,128},{8,136},{16,144},{24,152},{32,160},{40,168},{48,176},{56,1... | collective-permute-start | bytes 147464 | tf_op jit(solution)/shard_map/ppermute | solution.py:393
  38.1 0.9 %collective-permute-start.2 = (bf16[96,256]{1,0:T(8,128)(2,1)S(1)}, bf16[96,256]{1,0:T(8,128)(2,1)S(1)}, u32[]{:S(2)}, u32[]{:S(2)}) collective-permute-start(bf16[96,256]{1,0:T(8,128)(2,1)S(1)} %get-tuple-element.36), channel_id=1, source_target_pairs={{0,64},{8,72},{16,80},{24,88},{32,96},{40,104},{48,112},{56,120},{... | collective-permute-start | bytes 147464 | tf_op jit(solution)/shard_map/ppermute | solution.py:393
  39.0 0.1 collective-permute-done.4.three_ref
  39.1 3.8 %collective-permute-done.3.two_ref = bf16[96,256]{1,0:T(8,128)(2,1)S(1)} collective-permute-done((bf16[96,256]{1,0:T(8,128)(2,1)S(1)}, bf16[96,256]{1,0:T(8,128)(2,1)S(1)}, u32[]{:S(2)}, u32[]{:S(2)}) %collective-permute-start.3) | collective-permute-done | bytes 49184 | tf_op jit(solution)/shard_map/ppermute | solution.py:393
  42.9 0.5 collective-permute-done.2.one_ref
  43.4 0.1 state.1
  43.5 1.9 %collective-permute-start.6 = (bf16[512,256]{1,0:T(8,128)(2,1)S(1)}, bf16[512,256]{1,0:T(8,128)(2,1)S(1)}, u32[]{:S(2)}, u32[]{:S(2)}) collective-permute-start(bf16[512,256]{1,0:T(8,128)(2,1)S(1)} %get-tuple-element.38.refs_1_), channel_id=1, source_target_pairs={{1,2},{2,1},{3,4},{4,3},{5,6},{6,5},{9,10},{10,9},{11,12},{12,11},... | collective-permute-start | bytes 786440 | tf_op jit(solution)/shard_map/ppermute | solution.py:384
  45.4 1.8 %collective-permute-start.5 = (bf16[512,256]{1,0:T(8,128)(2,1)S(1)}, bf16[512,256]{1,0:T(8,128)(2,1)S(1)}, u32[]{:S(2)}, u32[]{:S(2)}) collective-permute-start(bf16[512,256]{1,0:T(8,128)(2,1)S(1)} %get-tuple-element.38.refs_1_), channel_id=1, source_target_pairs={{0,1},{1,0},{2,3},{3,2},{4,5},{5,4},{6,7},{7,6},{8,9},{9,8},{10,11... | collective-permute-start | bytes 786440 | tf_op jit(solution)/shard_map/ppermute | solution.py:385
  47.2 0.1 tune.1
  47.3 3.9 %collective-permute-done.6.refs_2_ = bf16[512,256]{1,0:T(8,128)(2,1)S(1)} collective-permute-done((bf16[512,256]{1,0:T(8,128)(2,1)S(1)}, bf16[512,256]{1,0:T(8,128)(2,1)S(1)}, u32[]{:S(2)}, u32[]{:S(2)}) %collective-permute-start.6) | collective-permute-done | bytes 262176 | tf_op jit(solution)/shard_map/ppermute | solution.py:384
  51.2 0.0 collective-permute-done.5.refs_0_
  51.2 3.5 %second.1 = (f32[256,256]{1,0:T(8,128)S(1)}, f32[32,256]{1,0:T(8,128)S(1)}) custom-call(bf16[512,256]{1,0:T(8,128)(2,1)S(1)} %collective-permute-done.5.refs_0_, bf16[512,256]{1,0:T(8,128)(2,1)S(1)} %get-tuple-element.38.refs_1_, bf16[512,256]{1,0:T(8,128)(2,1)S(1)} %collective-permute-done.6.refs_2_, bf16[64,240]{1,0:T(8,128)(2,1)S(1)} %get-tuple-element.40.refs_3_, ...), custom_call_target="tpu_custom_call" | custom-call | tf_op jit(solution)/shard_map/second/pallas_call | solution.py:366
  54.7 0.6 collective-permute-start.9
  55.3 1.2 %collective-permute-start.8 = (f32[32,256]{1,0:T(8,128)S(1)}, f32[32,256]{1,0:T(8,128)S(1)}, u32[]{:S(2)}, u32[]{:S(2)}) collective-permute-start(f32[32,256]{1,0:T(8,128)S(1)} %get-tuple-element.43), channel_id=1, source_target_pairs={{0,128},{8,136},{16,144},{24,152},{32,160},{40,168},{48,176},{56,1... | collective-permute-start | bytes 98312 | tf_op jit(solution)/shard_map/ppermute | solution.py:393
  56.4 1.2 %collective-permute-start.7 = (f32[32,256]{1,0:T(8,128)S(1)}, f32[32,256]{1,0:T(8,128)S(1)}, u32[]{:S(2)}, u32[]{:S(2)}) collective-permute-start(f32[32,256]{1,0:T(8,128)S(1)} %get-tuple-element.43), channel_id=1, source_target_pairs={{0,64},{8,72},{16,80},{24,88},{32,96},{40,104},{48,112},{56,120},{... | collective-permute-start | bytes 98312 | tf_op jit(solution)/shard_map/ppermute | solution.py:393
  57.6 1.1 %collective-permute-done.9.three_ref = f32[32,256]{1,0:T(8,128)S(1)} collective-permute-done((f32[32,256]{1,0:T(8,128)S(1)}, f32[32,256]{1,0:T(8,128)S(1)}, u32[]{:S(2)}, u32[]{:S(2)}) %collective-permute-start.9) | collective-permute-done | bytes 32800 | tf_op jit(solution)/shard_map/ppermute | solution.py:393
  58.7 2.0 %collective-permute-done.8.two_ref = f32[32,256]{1,0:T(8,128)S(1)} collective-permute-done((f32[32,256]{1,0:T(8,128)S(1)}, f32[32,256]{1,0:T(8,128)S(1)}, u32[]{:S(2)}, u32[]{:S(2)}) %collective-permute-start.8) | collective-permute-done | bytes 32800 | tf_op jit(solution)/shard_map/ppermute | solution.py:393
  60.7 0.9 %collective-permute-done.7.one_ref = f32[32,256]{1,0:T(8,128)S(1)} collective-permute-done((f32[32,256]{1,0:T(8,128)S(1)}, f32[32,256]{1,0:T(8,128)S(1)}, u32[]{:S(2)}, u32[]{:S(2)}) %collective-permute-start.7) | collective-permute-done | bytes 32800 | tf_op jit(solution)/shard_map/ppermute | solution.py:393
  61.6 13.6 %all_to_all.11 = f32[8,32,256]{2,1,0:T(8,128)S(1)} all-to-all(f32[8,32,256]{2,1,0:T(8,128)S(1)} %bitcast.19), channel_id=1, replica_groups={{0,8,16,24,32,40,48,56},{64,72,80,88,96,104,112,120},{128,136,144,152,1..., dimensions={0} | all-to-all | bytes 524288 | tf_op jit(solution)/shard_map/all_to_all | solution.py:389
  75.2 0.8 final.1
  (1 shorter events, 0.0 us)
Async XLA Ops:
  1.4 6.3 %collective-permute-start.1 = (bf16[256,256]{1,0:T(8,128)(2,1)S(1)}, bf16[256,256]{1,0:T(8,128)(2,1)S(1)}, u32[]{:S(2)}, u32[]{:S(2)}) collective-permute-start(bf16[256,256]{1,0:T(8,128)(2,1)S(1)} %get-tuple-element.26.refs_1_), channel_id=1, source_target_pairs={{1,2},{2,1},{3,4},{4,3},{5,6},{6,5},{9,10},{10,9},{11,12},{12,11},... | collective-permute-start | bytes 393224 | tf_op jit(solution)/shard_map/ppermute | solution.py:384
  3.4 4.4 %collective-permute-start = (bf16[256,256]{1,0:T(8,128)(2,1)S(1)}, bf16[256,256]{1,0:T(8,128)(2,1)S(1)}, u32[]{:S(2)}, u32[]{:S(2)}) collective-permute-start(bf16[256,256]{1,0:T(8,128)(2,1)S(1)} %get-tuple-element.26.refs_1_), channel_id=1, source_target_pairs={{0,1},{1,0},{2,3},{3,2},{4,5},{5,4},{6,7},{7,6},{8,9},{9,8},{10,11... | collective-permute-start | bytes 393224 | tf_op jit(solution)/shard_map/ppermute | solution.py:385
  34.5 4.6 %collective-permute-start.4 = (bf16[96,256]{1,0:T(8,128)(2,1)S(1)}, bf16[96,256]{1,0:T(8,128)(2,1)S(1)}, u32[]{:S(2)}, u32[]{:S(2)}) collective-permute-start(bf16[96,256]{1,0:T(8,128)(2,1)S(1)} %get-tuple-element.36), channel_id=1, source_target_pairs={{0,192},{8,200},{16,208},{24,216},{32,224},{40,232},{48,240},{56,2... | collective-permute-start | bytes 147464 | tf_op jit(solution)/shard_map/ppermute | solution.py:393
  37.3 5.6 %collective-permute-start.3 = (bf16[96,256]{1,0:T(8,128)(2,1)S(1)}, bf16[96,256]{1,0:T(8,128)(2,1)S(1)}, u32[]{:S(2)}, u32[]{:S(2)}) collective-permute-start(bf16[96,256]{1,0:T(8,128)(2,1)S(1)} %get-tuple-element.36), channel_id=1, source_target_pairs={{0,128},{8,136},{16,144},{24,152},{32,160},{40,168},{48,176},{56,1... | collective-permute-start | bytes 147464 | tf_op jit(solution)/shard_map/ppermute | solution.py:393
  38.1 5.3 %collective-permute-start.2 = (bf16[96,256]{1,0:T(8,128)(2,1)S(1)}, bf16[96,256]{1,0:T(8,128)(2,1)S(1)}, u32[]{:S(2)}, u32[]{:S(2)}) collective-permute-start(bf16[96,256]{1,0:T(8,128)(2,1)S(1)} %get-tuple-element.36), channel_id=1, source_target_pairs={{0,64},{8,72},{16,80},{24,88},{32,96},{40,104},{48,112},{56,120},{... | collective-permute-start | bytes 147464 | tf_op jit(solution)/shard_map/ppermute | solution.py:393
  43.5 7.7 %collective-permute-start.6 = (bf16[512,256]{1,0:T(8,128)(2,1)S(1)}, bf16[512,256]{1,0:T(8,128)(2,1)S(1)}, u32[]{:S(2)}, u32[]{:S(2)}) collective-permute-start(bf16[512,256]{1,0:T(8,128)(2,1)S(1)} %get-tuple-element.38.refs_1_), channel_id=1, source_target_pairs={{1,2},{2,1},{3,4},{4,3},{5,6},{6,5},{9,10},{10,9},{11,12},{12,11},... | collective-permute-start | bytes 786440 | tf_op jit(solution)/shard_map/ppermute | solution.py:384
  45.4 5.8 %collective-permute-start.5 = (bf16[512,256]{1,0:T(8,128)(2,1)S(1)}, bf16[512,256]{1,0:T(8,128)(2,1)S(1)}, u32[]{:S(2)}, u32[]{:S(2)}) collective-permute-start(bf16[512,256]{1,0:T(8,128)(2,1)S(1)} %get-tuple-element.38.refs_1_), channel_id=1, source_target_pairs={{0,1},{1,0},{2,3},{3,2},{4,5},{5,4},{6,7},{7,6},{8,9},{9,8},{10,11... | collective-permute-start | bytes 786440 | tf_op jit(solution)/shard_map/ppermute | solution.py:385
  54.7 4.1 %collective-permute-start.9 = (f32[32,256]{1,0:T(8,128)S(1)}, f32[32,256]{1,0:T(8,128)S(1)}, u32[]{:S(2)}, u32[]{:S(2)}) collective-permute-start(f32[32,256]{1,0:T(8,128)S(1)} %get-tuple-element.43), channel_id=1, source_target_pairs={{0,192},{8,200},{16,208},{24,216},{32,224},{40,232},{48,240},{56,2... | collective-permute-start | bytes 98312 | tf_op jit(solution)/shard_map/ppermute | solution.py:393
  55.3 5.4 %collective-permute-start.8 = (f32[32,256]{1,0:T(8,128)S(1)}, f32[32,256]{1,0:T(8,128)S(1)}, u32[]{:S(2)}, u32[]{:S(2)}) collective-permute-start(f32[32,256]{1,0:T(8,128)S(1)} %get-tuple-element.43), channel_id=1, source_target_pairs={{0,128},{8,136},{16,144},{24,152},{32,160},{40,168},{48,176},{56,1... | collective-permute-start | bytes 98312 | tf_op jit(solution)/shard_map/ppermute | solution.py:393
  56.4 5.1 %collective-permute-start.7 = (f32[32,256]{1,0:T(8,128)S(1)}, f32[32,256]{1,0:T(8,128)S(1)}, u32[]{:S(2)}, u32[]{:S(2)}) collective-permute-start(f32[32,256]{1,0:T(8,128)S(1)} %get-tuple-element.43), channel_id=1, source_target_pairs={{0,64},{8,72},{16,80},{24,88},{32,96},{40,104},{48,112},{56,120},{... | collective-permute-start | bytes 98312 | tf_op jit(solution)/shard_map/ppermute | solution.py:393

commit v6 on v5

--- a/solution.py
+++ b/solution.py
@@ -171,10 +171,12 @@
 
 def slab_facts(slabs):
     slab = lax.axis_index("slab")
-    return slab % 2 == 1, (one_if(slab > 0), one_if(slab < slabs - 1))
-
-
-def six_planes(odd, paired, own, crossed):
+    return (slab % 2 == 1, (slab > 0) & (slab < slabs - 1)), (one_if(slab > 0), one_if(slab < slabs - 1))
+
+
+def six_planes(place, paired, own, crossed):
+    odd, between = place
+    crossed = jnp.where(between, crossed, 0.0)
     below, above = jnp.where(odd, paired, crossed), jnp.where(odd, crossed, paired)
     return jnp.concatenate([below, own, above], axis=1)
 
@@ -184,7 +186,7 @@
     out_ref, taps, hidden,
 ):
     keeps = edge_masks()
-    odd, inside = slab_facts(slabs)
+    place, inside = slab_facts(slabs)
     kernel_in, kernel_out = kernel_in_ref[...], kernel_out_ref[...]
     eps = sum(params_ref[...].astype(F32)[row : row + 1, W:] for row in (3, 4, 5))
     eps = jnp.concatenate([eps, eps], axis=1)
@@ -201,7 +203,7 @@
 
     def load(pair):
         rows = slice(pair * 16, pair * 16 + 16)
-        both = six_planes(odd, *[ref[rows, :].astype(F32) for ref in (paired_ref, latent_ref, crossed_ref)])
+        both = six_planes(place, *[ref[rows, :].astype(F32) for ref in (paired_ref, latent_ref, crossed_ref)])
         for k in range(2):
             taps[1 + pair * 2 + k] = taps_of(both[k * C : k * C + C], keeps, chosen)
 
@@ -296,7 +298,7 @@
     sum_ref, total_ref, taps, hidden,
 ):
     keeps = edge_masks()
-    odd, inside = slab_facts(slabs)
+    place, inside = slab_facts(slabs)
     part = lax.axis_index("level") % GROUP
     exists = {0: one_if(part > 0), EXT - 3: one_if(part < GROUP - 1)}
     kernel_in, kernel_out = kernel_in_ref[...], kernel_out_ref[...]
@@ -306,7 +308,7 @@
     def load(level, pair):
         at = level * EDGE + pair * 16
         refs = (paired_ref, latent_ref, crossed_ref)
-        both = six_planes(odd, *[ref[at : at + 16, :].astype(F32) for ref in refs])
+        both = six_planes(place, *[ref[at : at + 16, :].astype(F32) for ref in refs])
         for k in range(2):
             taps[level * EXT + pair * 2 + k] = taps_of(both[k * C : k * C + C], keeps, chosen[level])
 
@@ -377,7 +379,7 @@
     slabs = lax.axis_size("slab")
     levels = lax.axis_size("level")
     pairs = [(i, i ^ 1) for i in range(slabs)]
-    crossings = [(i, j) for k in range(1, slabs - 1, 2) for i, j in ((k, k + 1), (k + 1, k))]
+    crossings = [(i, (i + (1 if i % 2 else -1)) % slabs) for i in range(slabs)]
     groups = [list(range(k, k + GROUP)) for k in range(0, levels, GROUP)]
 
     def neighbours(latent):

time: 76.5 us -> 73.5 us (0.961)
  starting transfers between devices: 14.9 us -> 11 us
    ppermute x2, starting transfers between devices: 3.84 us -> 0.19 us  [neighbours(): crossed = lax.ppermute(latent, 'slab', crossings)]
where the time goes in v6:
time: 73.5 us; the launch traced here: 72.3 us
  blocking collectives  37.5 us (51%)
  waiting for transfers between devices  13.1 us (18%)
  starting transfers between devices  11 us (15%)
  Pallas kernels  8.7 us (12%)
  between operations  2.01 us (3%)
    all_to_all x2, blocking collectives, exchange(): lax.all_to_all(parts, 'level', 0, 0, axis_index_groups=groups)  37.5 us
    pallas_call x9, Pallas kernels, call(): pl.pallas_call(kernel, out_shape=outs if len(outs) > 1 else outs[0], in_s...  8.7 us
    ppermute x6, waiting for transfers between devices, earlier_groups(): lax.ppermute(total, 'level', [(i, (i + k) % levels) for i in range(levels)])  8.36 us
    ppermute x6, starting transfers between devices, earlier_groups(): lax.ppermute(total, 'level', [(i, (i + k) % levels) for i in range(levels)])  7.49 us
    ppermute x2, waiting for transfers between devices, neighbours(): crossed = lax.ppermute(latent, 'slab', crossings)  4.71 us
    ppermute x2, starting transfers between devices, neighbours(): return (lax.ppermute(latent, 'slab', pairs), latent, crossed)  3.36 us
  transfers between devices with their start and end apart: 10, of which 8 were waited for; matrix products, arithmetic and copies ran while one was open for 0% of the time, Pallas kernels for 0%

profile of v6, /device:TPU:8, one launch (start us, length us, event | category | flops | bytes accessed | tf_op | source)
XLA Modules:
  0.0 72.3 jit_solution(8373231396919105850)
XLA Ops:
  0.0 1.4 %opening.1 = (bf16[256,256]{1,0:T(8,128)(2,1)S(1)}, f32[256,256]{1,0:T(8,128)S(1)}, f32[256,256]{1,0:T(8,128)S(1)}, f32[64,256]{1,0:T(8,128)S(1)}, bf16[64,240]{...) custom-call(f32[8,2,32,128]{3,2,1,0:T(8,128)} %bitcast.21, ...), custom_call_target="tpu_custom_call" | custom-call | tf_op jit(solution)/shard_map/opening/pallas_call | solution.py:368
  1.4 0.1 collective-permute-start.1
  1.5 1.7 %collective-permute-start = (bf16[256,256]{1,0:T(8,128)(2,1)S(1)}, bf16[256,256]{1,0:T(8,128)(2,1)S(1)}, u32[]{:S(2)}, u32[]{:S(2)}) collective-permute-start(bf16[256,256]{1,0:T(8,128)(2,1)S(1)} %get-tuple-element.26.refs_1_), channel_id=1, source_target_pairs={{0,1},{1,0},{2,3},{3,2},{4,5},{5,4},{6,7},{7,6},{8,9},{9,8},{10,11... | collective-permute-start | bytes 393224 | tf_op jit(solution)/shard_map/ppermute | solution.py:387
  5.2 0.1 prepare.1
  5.2 0.7 collective-permute-done.1.refs_2_
  5.9 0.0 collective-permute-done.refs_0_
  5.9 2.7 %first.1 = bf16[832,256]{1,0:T(8,128)(2,1)S(1)} custom-call(bf16[256,256]{1,0:T(8,128)(2,1)S(1)} %collective-permute-done.refs_0_, bf16[256,256]{1,0:T(8,128)(2,1)S(1)} %get-tuple-element.26.refs_1_, bf16[256,256]{1,0:T(8,128)(2,1)S(1)} %collective-permute-done.1.refs_2_, bf16[64,240]{1,0:T(8,128)(2,1)S(1)} %get-tuple-element.27.refs_3_, ...), custom_call_target="tpu_custom_call" | custom-call | tf_op jit(solution)/shard_map/first/pallas_call | solution.py:368
  8.7 23.9 %all_to_all.10 = bf16[8,104,256]{2,1,0:T(8,128)(2,1)S(1)} all-to-all(bf16[8,104,256]{2,1,0:T(8,128)(2,1)S(1)} %bitcast.18), channel_id=1, replica_groups={{0,8,16,24,32,40,48,56},{64,72,80,88,96,104,112,120},{128,136,144,152,1..., dimensions={0} | all-to-all | bytes 851968 | tf_op jit(solution)/shard_map/all_to_all | solution.py:391
  32.6 0.1 scan.1
  32.7 2.8 %collective-permute-start.4 = (bf16[96,256]{1,0:T(8,128)(2,1)S(1)}, bf16[96,256]{1,0:T(8,128)(2,1)S(1)}, u32[]{:S(2)}, u32[]{:S(2)}) collective-permute-start(bf16[96,256]{1,0:T(8,128)(2,1)S(1)} %get-tuple-element.36), channel_id=1, source_target_pairs={{0,192},{8,200},{16,208},{24,216},{32,224},{40,232},{48,240},{56,2... | collective-permute-start | bytes 147464 | tf_op jit(solution)/shard_map/ppermute | solution.py:395
  35.5 0.8 %collective-permute-start.3 = (bf16[96,256]{1,0:T(8,128)(2,1)S(1)}, bf16[96,256]{1,0:T(8,128)(2,1)S(1)}, u32[]{:S(2)}, u32[]{:S(2)}) collective-permute-start(bf16[96,256]{1,0:T(8,128)(2,1)S(1)} %get-tuple-element.36), channel_id=1, source_target_pairs={{0,128},{8,136},{16,144},{24,152},{32,160},{40,168},{48,176},{56,1... | collective-permute-start | bytes 147464 | tf_op jit(solution)/shard_map/ppermute | solution.py:395
  36.3 0.9 %collective-permute-start.2 = (bf16[96,256]{1,0:T(8,128)(2,1)S(1)}, bf16[96,256]{1,0:T(8,128)(2,1)S(1)}, u32[]{:S(2)}, u32[]{:S(2)}) collective-permute-start(bf16[96,256]{1,0:T(8,128)(2,1)S(1)} %get-tuple-element.36), channel_id=1, source_target_pairs={{0,64},{8,72},{16,80},{24,88},{32,96},{40,104},{48,112},{56,120},{... | collective-permute-start | bytes 147464 | tf_op jit(solution)/shard_map/ppermute | solution.py:395
  37.2 0.1 collective-permute-done.4.three_ref
  37.3 3.8 %collective-permute-done.3.two_ref = bf16[96,256]{1,0:T(8,128)(2,1)S(1)} collective-permute-done((bf16[96,256]{1,0:T(8,128)(2,1)S(1)}, bf16[96,256]{1,0:T(8,128)(2,1)S(1)}, u32[]{:S(2)}, u32[]{:S(2)}) %collective-permute-start.3) | collective-permute-done | bytes 49184 | tf_op jit(solution)/shard_map/ppermute | solution.py:395
  41.1 0.5 collective-permute-done.2.one_ref
  41.6 0.1 state.1
  41.7 0.1 collective-permute-start.6
  41.8 1.7 %collective-permute-start.5 = (bf16[512,256]{1,0:T(8,128)(2,1)S(1)}, bf16[512,256]{1,0:T(8,128)(2,1)S(1)}, u32[]{:S(2)}, u32[]{:S(2)}) collective-permute-start(bf16[512,256]{1,0:T(8,128)(2,1)S(1)} %get-tuple-element.38.refs_1_), channel_id=1, source_target_pairs={{0,1},{1,0},{2,3},{3,2},{4,5},{5,4},{6,7},{7,6},{8,9},{9,8},{10,11... | collective-permute-start | bytes 786440 | tf_op jit(solution)/shard_map/ppermute | solution.py:387
  43.5 0.1 tune.1
  43.6 4.0 %collective-permute-done.6.refs_2_ = bf16[512,256]{1,0:T(8,128)(2,1)S(1)} collective-permute-done((bf16[512,256]{1,0:T(8,128)(2,1)S(1)}, bf16[512,256]{1,0:T(8,128)(2,1)S(1)}, u32[]{:S(2)}, u32[]{:S(2)}) %collective-permute-start.6) | collective-permute-done | bytes 262176 | tf_op jit(solution)/shard_map/ppermute | solution.py:386
  47.6 0.0 collective-permute-done.5.refs_0_
  47.6 3.5 %second.1 = (f32[256,256]{1,0:T(8,128)S(1)}, f32[32,256]{1,0:T(8,128)S(1)}) custom-call(bf16[512,256]{1,0:T(8,128)(2,1)S(1)} %collective-permute-done.5.refs_0_, bf16[512,256]{1,0:T(8,128)(2,1)S(1)} %get-tuple-element.38.refs_1_, bf16[512,256]{1,0:T(8,128)(2,1)S(1)} %collective-permute-done.6.refs_2_, bf16[64,240]{1,0:T(8,128)(2,1)S(1)} %get-tuple-element.40.refs_3_, ...), custom_call_target="tpu_custom_call" | custom-call | tf_op jit(solution)/shard_map/second/pallas_call | solution.py:368
  51.1 0.6 collective-permute-start.9
  51.7 1.2 %collective-permute-start.8 = (f32[32,256]{1,0:T(8,128)S(1)}, f32[32,256]{1,0:T(8,128)S(1)}, u32[]{:S(2)}, u32[]{:S(2)}) collective-permute-start(f32[32,256]{1,0:T(8,128)S(1)} %get-tuple-element.43), channel_id=1, source_target_pairs={{0,128},{8,136},{16,144},{24,152},{32,160},{40,168},{48,176},{56,1... | collective-permute-start | bytes 98312 | tf_op jit(solution)/shard_map/ppermute | solution.py:395
  52.8 1.2 %collective-permute-start.7 = (f32[32,256]{1,0:T(8,128)S(1)}, f32[32,256]{1,0:T(8,128)S(1)}, u32[]{:S(2)}, u32[]{:S(2)}) collective-permute-start(f32[32,256]{1,0:T(8,128)S(1)} %get-tuple-element.43), channel_id=1, source_target_pairs={{0,64},{8,72},{16,80},{24,88},{32,96},{40,104},{48,112},{56,120},{... | collective-permute-start | bytes 98312 | tf_op jit(solution)/shard_map/ppermute | solution.py:395
  54.0 1.1 %collective-permute-done.9.three_ref = f32[32,256]{1,0:T(8,128)S(1)} collective-permute-done((f32[32,256]{1,0:T(8,128)S(1)}, f32[32,256]{1,0:T(8,128)S(1)}, u32[]{:S(2)}, u32[]{:S(2)}) %collective-permute-start.9) | collective-permute-done | bytes 32800 | tf_op jit(solution)/shard_map/ppermute | solution.py:395
  55.1 2.0 %collective-permute-done.8.two_ref = f32[32,256]{1,0:T(8,128)S(1)} collective-permute-done((f32[32,256]{1,0:T(8,128)S(1)}, f32[32,256]{1,0:T(8,128)S(1)}, u32[]{:S(2)}, u32[]{:S(2)}) %collective-permute-start.8) | collective-permute-done | bytes 32800 | tf_op jit(solution)/shard_map/ppermute | solution.py:395
  57.1 0.9 %collective-permute-done.7.one_ref = f32[32,256]{1,0:T(8,128)S(1)} collective-permute-done((f32[32,256]{1,0:T(8,128)S(1)}, f32[32,256]{1,0:T(8,128)S(1)}, u32[]{:S(2)}, u32[]{:S(2)}) %collective-permute-start.7) | collective-permute-done | bytes 32800 | tf_op jit(solution)/shard_map/ppermute | solution.py:395
  58.0 13.6 %all_to_all.11 = f32[8,32,256]{2,1,0:T(8,128)S(1)} all-to-all(f32[8,32,256]{2,1,0:T(8,128)S(1)} %bitcast.19), channel_id=1, replica_groups={{0,8,16,24,32,40,48,56},{64,72,80,88,96,104,112,120},{128,136,144,152,1..., dimensions={0} | all-to-all | bytes 524288 | tf_op jit(solution)/shard_map/all_to_all | solution.py:391
  71.6 0.8 %final.1 = f32[8,2,32,128]{3,2,1,0:T(8,128)} custom-call(f32[256,256]{1,0:T(8,128)S(1)} %bitcast.20), custom_call_target="tpu_custom_call" | custom-call | tf_op jit(solution)/shard_map/final/pallas_call | solution.py:368
  (1 shorter events, 0.0 us)
Async XLA Ops:
  1.4 4.5 %collective-permute-start.1 = (bf16[256,256]{1,0:T(8,128)(2,1)S(1)}, bf16[256,256]{1,0:T(8,128)(2,1)S(1)}, u32[]{:S(2)}, u32[]{:S(2)}) collective-permute-start(bf16[256,256]{1,0:T(8,128)(2,1)S(1)} %get-tuple-element.26.refs_1_), channel_id=1, source_target_pairs={{0,7},{1,2},{2,1},{3,4},{4,3},{5,6},{6,5},{7,0},{8,15},{9,10},{10,... | collective-permute-start | bytes 393224 | tf_op jit(solution)/shard_map/ppermute | solution.py:386
  1.5 4.4 %collective-permute-start = (bf16[256,256]{1,0:T(8,128)(2,1)S(1)}, bf16[256,256]{1,0:T(8,128)(2,1)S(1)}, u32[]{:S(2)}, u32[]{:S(2)}) collective-permute-start(bf16[256,256]{1,0:T(8,128)(2,1)S(1)} %get-tuple-element.26.refs_1_), channel_id=1, source_target_pairs={{0,1},{1,0},{2,3},{3,2},{4,5},{5,4},{6,7},{7,6},{8,9},{9,8},{10,11... | collective-permute-start | bytes 393224 | tf_op jit(solution)/shard_map/ppermute | solution.py:387
  32.7 4.6 %collective-permute-start.4 = (bf16[96,256]{1,0:T(8,128)(2,1)S(1)}, bf16[96,256]{1,0:T(8,128)(2,1)S(1)}, u32[]{:S(2)}, u32[]{:S(2)}) collective-permute-start(bf16[96,256]{1,0:T(8,128)(2,1)S(1)} %get-tuple-element.36), channel_id=1, source_target_pairs={{0,192},{8,200},{16,208},{24,216},{32,224},{40,232},{48,240},{56,2... | collective-permute-start | bytes 147464 | tf_op jit(solution)/shard_map/ppermute | solution.py:395
  35.5 5.6 %collective-permute-start.3 = (bf16[96,256]{1,0:T(8,128)(2,1)S(1)}, bf16[96,256]{1,0:T(8,128)(2,1)S(1)}, u32[]{:S(2)}, u32[]{:S(2)}) collective-permute-start(bf16[96,256]{1,0:T(8,128)(2,1)S(1)} %get-tuple-element.36), channel_id=1, source_target_pairs={{0,128},{8,136},{16,144},{24,152},{32,160},{40,168},{48,176},{56,1... | collective-permute-start | bytes 147464 | tf_op jit(solution)/shard_map/ppermute | solution.py:395
  36.3 5.3 %collective-permute-start.2 = (bf16[96,256]{1,0:T(8,128)(2,1)S(1)}, bf16[96,256]{1,0:T(8,128)(2,1)S(1)}, u32[]{:S(2)}, u32[]{:S(2)}) collective-permute-start(bf16[96,256]{1,0:T(8,128)(2,1)S(1)} %get-tuple-element.36), channel_id=1, source_target_pairs={{0,64},{8,72},{16,80},{24,88},{32,96},{40,104},{48,112},{56,120},{... | collective-permute-start | bytes 147464 | tf_op jit(solution)/shard_map/ppermute | solution.py:395
  41.7 5.9 %collective-permute-start.6 = (bf16[512,256]{1,0:T(8,128)(2,1)S(1)}, bf16[512,256]{1,0:T(8,128)(2,1)S(1)}, u32[]{:S(2)}, u32[]{:S(2)}) collective-permute-start(bf16[512,256]{1,0:T(8,128)(2,1)S(1)} %get-tuple-element.38.refs_1_), channel_id=1, source_target_pairs={{0,7},{1,2},{2,1},{3,4},{4,3},{5,6},{6,5},{7,0},{8,15},{9,10},{10,... | collective-permute-start | bytes 786440 | tf_op jit(solution)/shard_map/ppermute | solution.py:386
  41.8 5.8 %collective-permute-start.5 = (bf16[512,256]{1,0:T(8,128)(2,1)S(1)}, bf16[512,256]{1,0:T(8,128)(2,1)S(1)}, u32[]{:S(2)}, u32[]{:S(2)}) collective-permute-start(bf16[512,256]{1,0:T(8,128)(2,1)S(1)} %get-tuple-element.38.refs_1_), channel_id=1, source_target_pairs={{0,1},{1,0},{2,3},{3,2},{4,5},{5,4},{6,7},{7,6},{8,9},{9,8},{10,11... | collective-permute-start | bytes 786440 | tf_op jit(solution)/shard_map/ppermute | solution.py:387
  51.1 4.1 %collective-permute-start.9 = (f32[32,256]{1,0:T(8,128)S(1)}, f32[32,256]{1,0:T(8,128)S(1)}, u32[]{:S(2)}, u32[]{:S(2)}) collective-permute-start(f32[32,256]{1,0:T(8,128)S(1)} %get-tuple-element.43), channel_id=1, source_target_pairs={{0,192},{8,200},{16,208},{24,216},{32,224},{40,232},{48,240},{56,2... | collective-permute-start | bytes 98312 | tf_op jit(solution)/shard_map/ppermute | solution.py:395
  51.7 5.4 %collective-permute-start.8 = (f32[32,256]{1,0:T(8,128)S(1)}, f32[32,256]{1,0:T(8,128)S(1)}, u32[]{:S(2)}, u32[]{:S(2)}) collective-permute-start(f32[32,256]{1,0:T(8,128)S(1)} %get-tuple-element.43), channel_id=1, source_target_pairs={{0,128},{8,136},{16,144},{24,152},{32,160},{40,168},{48,176},{56,1... | collective-permute-start | bytes 98312 | tf_op jit(solution)/shard_map/ppermute | solution.py:395
  52.8 5.1 %collective-permute-start.7 = (f32[32,256]{1,0:T(8,128)S(1)}, f32[32,256]{1,0:T(8,128)S(1)}, u32[]{:S(2)}, u32[]{:S(2)}) collective-permute-start(f32[32,256]{1,0:T(8,128)S(1)} %get-tuple-element.43), channel_id=1, source_target_pairs={{0,64},{8,72},{16,80},{24,88},{32,96},{40,104},{48,112},{56,120},{... | collective-permute-start | bytes 98312 | tf_op jit(solution)/shard_map/ppermute | solution.py:395
